TPU v7x, 256 devices: a whole 4x4x8 slice. The times are simulated.
256 devices in a mesh: dp: 8 (over y, core), proto: 32 (over z, x).
Axes of the slice: x: 4, y: 4, z: 8, core: 2. Of those that a mesh axis runs over, the one named last changes fastest.
Arguments:
- teacher_features: bfloat16 [6144, 384], P('dp'), may hold values from -8 to 8
- student_features: bfloat16 [6144, 384], P('dp'), may hold values from -8 to 8
- teacher_weight: bfloat16 [384, 131072], P('dp', 'proto'), may hold values from -1 to 1
- student_weight: bfloat16 [384, 131072], P('dp', 'proto'), may hold values from -1 to 1
Outputs:
- teacher_codes: bfloat16 [6144, 131072], P('dp', 'proto')
- head_loss: float32 [], replicated
- weight_grad: float32 [384, 131072], P('dp', 'proto')
All inputs are finite; a program needn't handle non-finite values.
Results may differ from a plain program's by a relative error of at most 0.003.
Values may be sent and summed in bfloat16 or wider, within the bound.
A program may use at most 128 MiB of HBM per device.

v0:
```python
import jax
import jax.numpy as jnp
from jax import lax
from jax.sharding import PartitionSpec as P

ITERS = 3


teacher_temp = 0.07
student_temp = 0.1
norm_eps = 1e-06


def column_norm(weight_rows):
    return jnp.sqrt(jnp.sum(jnp.square(weight_rows.astype(jnp.float32)), axis=0) + norm_eps)


def body(teacher_features, student_features, teacher_weight, student_weight):
    local_crops = teacher_features.shape[0]
    total_crops = local_crops * lax.axis_size("dp")
    total_protos = teacher_weight.shape[1] * lax.axis_size("proto")
    teacher_full, student_full = (
        lax.all_gather(teacher_weight, "dp", axis=0, tiled=True),
        lax.all_gather(student_weight, "dp", axis=0, tiled=True),
    )
    teacher_norm = column_norm(teacher_full)
    student_norm = column_norm(student_full)
    teacher_logits = (
        jnp.dot(teacher_features, teacher_full, preferred_element_type=jnp.float32) / teacher_norm
    )
    student_logits = (
        jnp.dot(student_features, student_full, preferred_element_type=jnp.float32) / student_norm
    )
    teacher_peak, student_peak = lax.pmax(
        (jnp.max(teacher_logits, axis=1), jnp.max(student_logits, axis=1)), "proto"
    )
    powers = jnp.exp((teacher_logits - teacher_peak[:, None]) / teacher_temp)
    shifted = (student_logits - student_peak[:, None]) / student_temp
    student_local = jnp.sum(jnp.exp(shifted), axis=1)
    crop_scale = jnp.ones((local_crops,), jnp.float32)
    for sweep_index in range(ITERS):
        proto_mass = lax.psum(jnp.dot(crop_scale, powers, precision=lax.Precision.HIGHEST), "dp")
        proto_scale = 1.0 / (total_protos * proto_mass)
        crop_local = jnp.dot(powers, proto_scale, precision=lax.Precision.HIGHEST)
        if sweep_index == 0:
            crop_mass = lax.psum(crop_local, "proto")
        else:
            crop_mass = lax.psum(crop_local, "proto")
        crop_scale = 1.0 / (total_crops * crop_mass)
    student_total = lax.psum(student_local, "proto")
    assign = powers * proto_scale[None, :] * crop_scale[:, None] * total_crops
    teacher_codes = assign.astype(jnp.bfloat16)
    log_prob = shifted - jnp.log(student_total)[:, None]
    loss_local = -jnp.sum(assign * log_prob)
    signal = ((jnp.exp(log_prob) - assign) / student_temp).astype(jnp.bfloat16)
    head_loss = lax.psum(loss_local, ("dp", "proto")) / total_crops
    own_weight = student_weight.astype(jnp.float32) / student_norm
    own_grad = lax.psum_scatter(
        lax.dot_general(
            student_features, signal, (((0,), (0,)), ((), ())), preferred_element_type=jnp.float32
        ),
        "dp",
        scatter_dimension=0,
        tiled=True,
    )
    pressure = lax.psum(jnp.sum(own_grad * own_weight, axis=0), "dp")
    weight_grad = (own_grad - own_weight * pressure[None, :]) / student_norm
    return (teacher_codes, head_loss, weight_grad)


def solution(mesh):
    return jax.shard_map(
        body,
        mesh=mesh,
        in_specs=(P("dp", None), P("dp", None), P("dp", "proto"), P("dp", "proto")),
        out_specs=(P("dp", "proto"), P(), P("dp", "proto")),
        check_vma=False,
    )
```

profile of v0, /device:TPU:1, one launch (start us, length us, event | category | flops | bytes accessed | tf_op | source)
XLA Modules:
  0.0 682.7 jit_solution(6292353373318271310)
XLA Ops:
  7.2 0.0 copy-start
  7.2 0.0 all-gather.5.cloned.1.call-start
  7.2 0.7 all-gather.5.cloned.1.call-update
  7.9 0.0 all-gather.3.cloned.1.call-start
  8.0 0.7 all-gather.3.cloned.1.call-update
  8.7 0.0 reduce-scatter.4.cloned.1.call-start
  8.7 35.7 %all-gather.5.cloned.1.call-done = bf16[384,4096]{1,0:T(8,128)(2,1)} async-done(((bf16[48,4096]{1,0:T(8,128)(2,1)}), bf16[384,4096]{1,0:T(8,128)(2,1)}) %all-gather.5.cloned.1.call-update) | async-done | bytes 3145744 | tf_op jit(solution)/shard_map/all_gather | solution.py:24
  44.4 2.6 multiply_reduce_fusion.1
  47.0 29.6 %all-gather.3.cloned.1.call-done = bf16[384,4096]{1,0:T(8,128)(2,1)} async-done(((bf16[48,4096]{1,0:T(8,128)(2,1)}), bf16[384,4096]{1,0:T(8,128)(2,1)}) %all-gather.3.cloned.1.call-update) | async-done | bytes 3145744 | tf_op jit(solution)/shard_map/all_gather | solution.py:23
  76.7 2.6 multiply_reduce_fusion.2
  79.3 0.0 copy-done
  79.3 0.0 copy-start.2
  79.3 0.0 copy-start.4
  79.3 8.5 %fusion.9 = (f32[768]{0:T(1024)S(1)}, f32[768,4096]{1,0:T(8,128)}) fusion(f32[4096]{0:T(1024)S(1)} %add_sqrt_fusion, bf16[768,384]{1,0:T(8,128)(2,1)S(1)} %copy-done, bf16[384,4096]{1,0:T(8,128)(2,1)} %all-gather.5.cloned.1.call-done), kind=kOutput, calls=%fused_computation.33 | convolution fusion | flops 2422209792 | bytes 16337920 | tf_op jit(solution)/shard_map/dot_general | solution.py:32
  87.8 0.0 copy-done.2
  87.8 0.0 copy-done.4
  87.8 6.4 fusion.3
  94.2 62.7 %all-reduce.1 = (f32[768]{0:T(1024)S(1)}, f32[768]{0:T(1024)S(1)}) all-reduce(f32[768]{0:T(1024)S(1)} %get-tuple-element.15, f32[768]{0:T(1024)S(1)} %get-tuple-element.17), channel_id=1, replica_groups=mesh['dp'=8,'proto'=32] {'proto'}, use_global_device_ids=true, to_apply=%region_2.0 | all-reduce | flops 1536 | bytes 12288 | tf_op jit(solution)/shard_map/pmax | solution.py:34
  156.9 10.4 %exponential_reduce_fusion = (f32[768]{0:T(1024)S(1)}, f32[768,4096]{1,0:T(8,128)S(1)}) fusion(f32[768,4096]{1,0:T(8,128)} %get-tuple-element.18, f32[768]{0:T(1024)S(1)} %get-tuple-element.12, f32[768]{0:T(1024)S(1)} %get-tuple-element.11, f32[768,4096]{1,0:T(8,128)} %get-tuple-element.16, f32[4096]{0:T(1024)S(1)} %add_sqrt_fusion.1), kind=kLoop, calls=%fused_computation.2 | loop fusion | flops 18873600 | bytes 37774336 | tf_op jit(solution)/shard_map/reduce_sum | solution.py:39
  167.4 0.0 copy-start.1
  167.4 4.5 copy-done.1
  171.9 6.0 fusion.4
  177.8 34.4 %psum.63 = f32[4096]{0:T(1024)S(1)} all-reduce(f32[4096]{0:T(1024)S(1)} %bitcast.30), channel_id=1, replica_groups=mesh['dp'=8,'proto'=32] {'dp'}, use_global_device_ids=true, to_apply=%region_3.0 | all-reduce | flops 4096 | bytes 32768 | tf_op jit(solution)/shard_map/psum | solution.py:42
  212.2 13.3 %convolution_reduce_fusion.2 = f32[768]{0:T(1024)S(1)} fusion(f32[768,4096]{1,0:T(8,128)} %copy-done.1, f32[4096,1]{0,1:T(1,128)S(1)} %bitcast.26), kind=kOutput, calls=%fused_computation.19 | convolution fusion | flops 37748736 | bytes 12602368 | tf_op jit(solution)/shard_map/dot_general | solution.py:44
  225.5 55.8 %psum.64 = f32[768]{0:T(1024)S(1)} all-reduce(f32[768]{0:T(1024)S(1)} %convolution_reduce_fusion.2), channel_id=1, replica_groups=mesh['dp'=8,'proto'=32] {'proto'}, use_global_device_ids=true, to_apply=%region_4.0 | all-reduce | flops 768 | bytes 6144 | tf_op jit(solution)/shard_map/psum | solution.py:46
  281.3 8.5 %fusion.10 = f32[1,4096]{1,0:T(1,128)S(1)} fusion(f32[768,1]{0,1:T(1,128)S(1)} %reshape.24, f32[768,4096]{1,0:T(8,128)} %copy-done.1), kind=kOutput, calls=%fused_computation.34 | convolution fusion | flops 37748736 | bytes 12602368 | tf_op jit(solution)/shard_map/dot_general | solution.py:42
  289.9 37.4 %psum.65 = f32[4096]{0:T(1024)S(1)} all-reduce(f32[4096]{0:T(1024)S(1)} %bitcast.27), channel_id=1, replica_groups=mesh['dp'=8,'proto'=32] {'dp'}, use_global_device_ids=true, to_apply=%region_5.0 | all-reduce | flops 4096 | bytes 32768 | tf_op jit(solution)/shard_map/psum | solution.py:42
  327.3 13.3 %convolution_reduce_fusion.1 = f32[768]{0:T(1024)S(1)} fusion(f32[768,4096]{1,0:T(8,128)} %copy-done.1, f32[4096,1]{0,1:T(1,128)S(1)} %bitcast.28), kind=kOutput, calls=%fused_computation.18 | convolution fusion | flops 37748736 | bytes 12602368 | tf_op jit(solution)/shard_map/dot_general | solution.py:44
  340.6 58.0 %psum.66 = f32[768]{0:T(1024)S(1)} all-reduce(f32[768]{0:T(1024)S(1)} %convolution_reduce_fusion.1), channel_id=1, replica_groups=mesh['dp'=8,'proto'=32] {'proto'}, use_global_device_ids=true, to_apply=%region_6.0 | all-reduce | flops 768 | bytes 6144 | tf_op jit(solution)/shard_map/psum | solution.py:48
  398.6 8.5 %fusion.11 = f32[1,4096]{1,0:T(1,128)S(1)} fusion(f32[768,1]{0,1:T(1,128)S(1)} %reshape.28, f32[768,4096]{1,0:T(8,128)} %copy-done.1), kind=kOutput, calls=%fused_computation.35 | convolution fusion | flops 37748736 | bytes 12602368 | tf_op jit(solution)/shard_map/dot_general | solution.py:42
  407.1 37.4 %psum.67 = f32[4096]{0:T(1024)S(1)} all-reduce(f32[4096]{0:T(1024)S(1)} %bitcast.29), channel_id=1, replica_groups=mesh['dp'=8,'proto'=32] {'dp'}, use_global_device_ids=true, to_apply=%region_7.0 | all-reduce | flops 4096 | bytes 32768 | tf_op jit(solution)/shard_map/psum | solution.py:42
  444.6 13.3 %convolution_reduce_fusion = f32[768]{0:T(1024)S(1)} fusion(f32[768,4096]{1,0:T(8,128)} %copy-done.1, f32[4096,1]{0,1:T(1,128)S(1)} %bitcast.25), kind=kOutput, calls=%fused_computation.17 | convolution fusion | flops 37748736 | bytes 12602368 | tf_op jit(solution)/shard_map/dot_general | solution.py:44
  457.9 57.0 %all-reduce = (f32[768]{0:T(1024)S(1)}, f32[768]{0:T(1024)S(1)}) all-reduce(f32[768]{0:T(1024)S(1)} %convolution_reduce_fusion, f32[768]{0:T(1024)S(1)} %get-tuple-element.19), channel_id=1, replica_groups=mesh['dp'=8,'proto'=32] {'proto'}, use_global_device_ids=true, to_apply=%region_8.0 | all-reduce | flops 1536 | bytes 12288 | tf_op jit(solution)/shard_map/psum | solution.py:48
  514.9 13.1 %fusion.2 = f32[384,4096]{0,1:T(8,128)} fusion(bf16[768,384]{1,0:T(8,128)(2,1)S(1)} %copy-done, f32[768,4096]{1,0:T(8,128)} %get-tuple-element.18, f32[768,4096]{1,0:T(8,128)} %copy-done.1, f32[768]{0:T(1024)S(1)} %log.3, f32[768]{0:T(1024)S(1)} %get-tuple-element.12, f32[768]{0:T(1024)S(1)} %multiply_divide_fusion.3, f32[4096]{0:T(1024)S(1)} %multiply_divide_fusion), kind=kOutput, calls=%fused_computation.12 | convolution fusion | flops 2444230656 | bytes 32072704 | tf_op jit(solution)/shard_map/dot_general | solution.py:59
  528.0 6.5 copy.11
  534.5 0.0 reduce-scatter.4.cloned.1.call-update
  534.5 0.0 copy-start.3
  534.5 14.4 %multiply_reduce_fusion = (f32[]{:T(128)}, bf16[768,4096]{1,0:T(8,128)(2,1)}) fusion(f32[768,4096]{1,0:T(8,128)} %get-tuple-element.18, f32[768,4096]{1,0:T(8,128)} %copy-done.1, f32[768]{0:T(1024)S(1)} %log.3, f32[768]{0:T(1024)S(1)} %get-tuple-element.12, f32[768]{0:T(1024)S(1)} %multiply_divide_fusion.3, f32[4096]{0:T(1024)S(1)} %multiply_divide_fusion), kind=kLoop, calls=%fused_computation.1 | loop fusion | flops 28311552 | bytes 31482884 | tf_op jit(solution)/shard_map/reduce_sum | solution.py:54
  549.6 0.0 copy-done.3
  549.6 1.3 copy.9
  550.9 90.5 %psum.70 = f32[]{:T(128)} all-reduce(f32[]{:T(128)S(6)} %neg.3), channel_id=1, replica_groups=mesh['dp'=8,'proto'=32] {'dp','proto'}, use_global_device_ids=true, to_apply=%region_15.0 | all-reduce | flops 1 | bytes 8 | tf_op jit(solution)/shard_map/psum | solution.py:56
  642.1 0.0 reduce-scatter.4.cloned.1.call-done
  642.1 1.7 copy.12
  643.9 2.3 multiply_reduce_fusion.3
  646.2 20.9 %psum.71 = f32[4096]{0:T(1024)S(1)} all-reduce(f32[4096]{0:T(1024)S(1)} %multiply_reduce_fusion.3), channel_id=1, replica_groups=mesh['dp'=8,'proto'=32] {'dp'}, use_global_device_ids=true, to_apply=%region_18.0 | all-reduce | flops 4096 | bytes 32768 | tf_op jit(solution)/shard_map/psum | solution.py:66
  667.1 4.6 subtract_divide_fusion
  671.7 3.1 copy.10
  (11 shorter events, 0.1 us)
Async XLA Ops:
  7.2 72.1 %copy-start = (bf16[768,384]{1,0:T(8,128)(2,1)S(1)}, bf16[768,384]{1,0:T(8,128)(2,1)}, u32[]{:S(2)}) copy-start(bf16[768,384]{1,0:T(8,128)(2,1)} %param.5) | copy-start | bytes 1769476
  7.2 37.3 %all-gather.5.cloned.1.call-start = ((), (), s32[]{:S(2)}) async-start(), calls=%async_computation.2 | async-start | bytes 3538944 | tf_op jit(solution)/shard_map/all_gather | solution.py:24
  7.9 68.8 %all-gather.3.cloned.1.call-start = ((), (), s32[]{:S(2)}) async-start(), calls=%async_computation.1 | async-start | bytes 3538944 | tf_op jit(solution)/shard_map/all_gather | solution.py:23
  8.7 633.5 %reduce-scatter.4.cloned.1.call-start = ((), (), s32[]{:S(2)}) async-start(), calls=%async_computation.3 | async-start | bytes 7077888
  79.3 8.6 %copy-start.2 = (bf16[384,4096]{1,0:T(8,128)(2,1)S(1)}, bf16[384,4096]{1,0:T(8,128)(2,1)}, u32[]{:S(2)}) copy-start(bf16[384,4096]{1,0:T(8,128)(2,1)} %all-gather.3.cloned.1.call-done) | copy-start | bytes 9437188
  79.3 8.6 %copy-start.4 = (bf16[768,384]{1,0:T(8,128)(2,1)S(1)}, bf16[768,384]{1,0:T(8,128)(2,1)}, u32[]{:S(2)}) copy-start(bf16[768,384]{1,0:T(8,128)(2,1)} %param.4) | copy-start | bytes 1769476
  167.4 4.5 copy-start.1
  534.5 15.1 %copy-start.3 = (bf16[48,4096]{1,0:T(8,128)(2,1)S(1)}, bf16[48,4096]{1,0:T(8,128)(2,1)}, u32[]{:S(2)}) copy-start(bf16[48,4096]{1,0:T(8,128)(2,1)} %param.7) | copy-start | bytes 1179652
Sparse Core Ops, SparseCore 0:
  9.8 34.5 all-gather.4
  46.3 30.3 all-gather.2
  534.7 56.8 reduce-scatter.3
where the time goes:
time: 689 us; the launch traced here: 683 us
  blocking collectives  454 us (66%)
  matrix products  91 us (13%)
  waiting for transfers between devices  66.8 us (10%)
  other arithmetic  37 us (5%)
  local copies, waits for them, and re-layouts  17.1 us (2%)
  between operations  16.6 us (2%)
    psum x3, blocking collectives, body(): crop_mass = lax.psum(crop_local, 'proto')  171 us
    psum x3, blocking collectives, body(): lax.psum(jnp.dot(crop_scale, powers, precision=lax.Precision.HIGHEST), 'dp')  109 us
    psum x1, blocking collectives, body(): head_loss = lax.psum(loss_local, ('dp', 'proto')) / total_crops  90.5 us
    pmax x1, blocking collectives, body(): lax.pmax((jnp.max(teacher_logits, axis=1), jnp.max(student_logits, axis=1...  62.7 us
    dot_general x3, matrix products, body(): crop_local = jnp.dot(powers, proto_scale, precision=lax.Precision.HIGHEST)  39.9 us
    all_gather x1, waiting for transfers between devices, body(): lax.all_gather(student_weight, 'dp', axis=0, tiled=True)  35.7 us
    all_gather x1, waiting for transfers between devices, body(): lax.all_gather(teacher_weight, 'dp', axis=0, tiled=True)  29.6 us
    dot_general x3, matrix products, body(): jnp.dot(crop_scale, powers, precision=lax.Precision.HIGHEST)  23 us
  transfers between devices with their start and end apart: 3, of which 2 were waited for; matrix products, arithmetic and copies ran while one was open for 3% of the time, Pallas kernels for 0%

commit v1 on v0

--- a/solution.py
+++ b/solution.py
@@ -1,6 +1,10 @@
+import functools
+
 import jax
 import jax.numpy as jnp
 from jax import lax
+from jax.experimental import pallas as pl
+from jax.experimental.pallas import tpu as pltpu
 from jax.sharding import PartitionSpec as P
 
 ITERS = 3
@@ -9,10 +13,65 @@
 teacher_temp = 0.07
 student_temp = 0.1
 norm_eps = 1e-06
+MESH = pl.DeviceIdType.MESH
+
+
+def exchange_kernel(axis, n, op, x_ref, o_ref, buf, send_sem, recv_sem):
+    me = lax.axis_index(axis)
+    barrier = pltpu.get_barrier_semaphore()
+
+    @pl.loop(1, n)
+    def _(o):
+        pl.semaphore_signal(barrier, inc=1, device_id={axis: lax.rem(me + o, n)}, device_id_type=MESH)
+
+    pl.semaphore_wait(barrier, n - 1)
+
+    @pl.loop(1, n)
+    def _(o):
+        pltpu.make_async_remote_copy(
+            src_ref=x_ref,
+            dst_ref=buf.at[o - 1],
+            send_sem=send_sem,
+            recv_sem=recv_sem,
+            device_id={axis: lax.rem(me + o, n)},
+            device_id_type=MESH,
+        ).start()
+
+    whole = pltpu.make_async_remote_copy(
+        src_ref=buf, dst_ref=buf, send_sem=send_sem, recv_sem=recv_sem,
+        device_id={axis: lax.rem(me + 1, n)}, device_id_type=MESH,
+    )
+    whole.wait_recv()
+    total = x_ref[...]
+    for o in range(1, n):
+        total = op(total, buf[o - 1])
+    o_ref[...] = total
+    whole.wait_send()
+
+
+def exchange(x, axis, op, collective_id):
+    n = lax.axis_size(axis)
+    rows = x.shape[0]
+    return pl.pallas_call(
+        functools.partial(exchange_kernel, axis, n, op),
+        out_shape=jax.ShapeDtypeStruct(x.shape, jnp.float32),
+        in_specs=[pl.BlockSpec(memory_space=pltpu.VMEM)],
+        out_specs=pl.BlockSpec(memory_space=pltpu.VMEM),
+        scratch_shapes=[
+            pltpu.VMEM((n - 1, rows, 128), jnp.float32),
+            pltpu.SemaphoreType.DMA,
+            pltpu.SemaphoreType.DMA,
+        ],
+        compiler_params=pltpu.CompilerParams(collective_id=collective_id, has_side_effects=True),
+    )(x)
 
 
 def column_norm(weight_rows):
     return jnp.sqrt(jnp.sum(jnp.square(weight_rows.astype(jnp.float32)), axis=0) + norm_eps)
+
+
+def pack(x):
+    return jnp.pad(x.reshape(6, 128), ((0, 2), (0, 0)))
 
 
 def body(teacher_features, student_features, teacher_weight, student_weight):
@@ -31,23 +90,26 @@
     student_logits = (
         jnp.dot(student_features, student_full, preferred_element_type=jnp.float32) / student_norm
     )
-    teacher_peak, student_peak = lax.pmax(
-        (jnp.max(teacher_logits, axis=1), jnp.max(student_logits, axis=1)), "proto"
+    peaks = exchange(
+        jnp.concatenate([pack(jnp.max(teacher_logits, axis=1)), pack(jnp.max(student_logits, axis=1))]),
+        "proto", jnp.maximum, 0,
     )
+    teacher_peak = peaks[:6].reshape(-1)
+    student_peak = peaks[8:14].reshape(-1)
     powers = jnp.exp((teacher_logits - teacher_peak[:, None]) / teacher_temp)
     shifted = (student_logits - student_peak[:, None]) / student_temp
     student_local = jnp.sum(jnp.exp(shifted), axis=1)
     crop_scale = jnp.ones((local_crops,), jnp.float32)
     for sweep_index in range(ITERS):
-        proto_mass = lax.psum(jnp.dot(crop_scale, powers, precision=lax.Precision.HIGHEST), "dp")
+        proto_mass = exchange(
+            jnp.sum(crop_scale[:, None] * powers, axis=0).reshape(32, 128), "dp", jnp.add, 1
+        ).reshape(-1)
         proto_scale = 1.0 / (total_protos * proto_mass)
-        crop_local = jnp.dot(powers, proto_scale, precision=lax.Precision.HIGHEST)
-        if sweep_index == 0:
-            crop_mass = lax.psum(crop_local, "proto")
-        else:
-            crop_mass = lax.psum(crop_local, "proto")
+        crop_local = jnp.sum(powers * proto_scale, axis=1)
+        sums = exchange(jnp.concatenate([pack(crop_local), pack(student_local)]), "proto", jnp.add, 2)
+        crop_mass = sums[:6].reshape(-1)
+        student_total = sums[8:14].reshape(-1)
         crop_scale = 1.0 / (total_crops * crop_mass)
-    student_total = lax.psum(student_local, "proto")
     assign = powers * proto_scale[None, :] * crop_scale[:, None] * total_crops
     teacher_codes = assign.astype(jnp.bfloat16)
     log_prob = shifted - jnp.log(student_total)[:, None]
@@ -63,7 +125,7 @@
         scatter_dimension=0,
         tiled=True,
     )
-    pressure = lax.psum(jnp.sum(own_grad * own_weight, axis=0), "dp")
+    pressure = exchange(jnp.sum(own_grad * own_weight, axis=0).reshape(32, 128), "dp", jnp.add, 1).reshape(-1)
     weight_grad = (own_grad - own_weight * pressure[None, :]) / student_norm
     return (teacher_codes, head_loss, weight_grad)
 

time: 689 us -> 374 us (0.54)
  blocking collectives: 454 us -> 77.2 us
  Pallas kernels: 0 us -> 90.1 us
  matrix products: 91 us -> 28 us
  other arithmetic: 37 us -> 80.6 us
    psum x7 -> x0, blocking collectives: 301 us -> none  [the longest x3 171 us: body(): crop_mass = lax.psum(crop_local, 'proto')]
    pallas_call x0 -> x8, Pallas kernels: none -> 90.1 us  [exchange(): pl.pallas_call(functools.partial(exchange_kernel, axis, n, op), out_shape...]
    dot_general x6 -> x0, matrix products: 62.9 us -> none  [the longest x3 39.9 us: body(): crop_local = jnp.dot(powers, proto_scale, precision=lax.Precision.HIGHEST)]
    pmax x1 -> x0, blocking collectives: 62.7 us -> none  [body(): lax.pmax((jnp.max(teacher_logits, axis=1), jnp.max(student_logits, axis=1...]
    reduce_sum x2 -> x7, other arithmetic: 12.8 us -> 49.1 us  [the longest x3 29.6 us: body(): jnp.sum(crop_scale[:, None] * powers, axis=0).reshape(32, 128)]
    psum x1, blocking collectives: 90.5 us -> 77.2 us  [body(): head_loss = lax.psum(loss_local, ('dp', 'proto')) / total_crops]
    unnamed x14 -> x12, local copies, waits for them, and re-layouts: 17.1 us -> 12.7 us
  transfers between devices with their start and end apart: 3 -> 3, of which waited for: 2 -> 2; matrix products, arithmetic and copies ran while one was open for 3% -> 5% of each run, Pallas kernels for 0% -> 0%
where the time goes in v1:
time: 374 us; the launch traced here: 372 us
  Pallas kernels  90.1 us (24%)
  other arithmetic  80.6 us (22%)
  blocking collectives  77.2 us (21%)
  waiting for transfers between devices  66.8 us (18%)
  matrix products  28 us (7%)
  between operations  16.3 us (4%)
  local copies, waits for them, and re-layouts  13.3 us (4%)
    pallas_call x8, Pallas kernels, exchange(): pl.pallas_call(functools.partial(exchange_kernel, axis, n, op), out_shape...  90.1 us
    psum x1, blocking collectives, body(): head_loss = lax.psum(loss_local, ('dp', 'proto')) / total_crops  77.2 us
    all_gather x1, waiting for transfers between devices, body(): lax.all_gather(student_weight, 'dp', axis=0, tiled=True)  35.7 us
    all_gather x1, waiting for transfers between devices, body(): lax.all_gather(teacher_weight, 'dp', axis=0, tiled=True)  29.6 us
    reduce_sum x3, other arithmetic, body(): jnp.sum(crop_scale[:, None] * powers, axis=0).reshape(32, 128)  29.6 us
    reduce_sum x3, other arithmetic, body(): crop_local = jnp.sum(powers * proto_scale, axis=1)  16.6 us
    reduce_sum x1, other arithmetic, body(): loss_local = -jnp.sum(assign * log_prob)  14.4 us
    dot_general x1, matrix products, body(): lax.dot_general(student_features, signal, (((0,), (0,)), ((), ())), prefe...  13.1 us
  transfers between devices with their start and end apart: 3, of which 2 were waited for; matrix products, arithmetic and copies ran while one was open for 5% of the time, Pallas kernels for 0%

profile of v1, /device:TPU:1, one launch (start us, length us, event | category | flops | bytes accessed | tf_op | source)
XLA Modules:
  0.0 372.5 jit_solution(16628047902778886627)
XLA Ops:
  7.2 0.0 copy-start
  7.2 0.0 all-gather.5.cloned.1.call-start
  7.2 0.7 all-gather.5.cloned.1.call-update
  7.9 0.0 all-gather.3.cloned.1.call-start
  8.0 0.7 all-gather.3.cloned.1.call-update
  8.7 0.0 reduce-scatter.4.cloned.1.call-start
  8.7 35.7 %all-gather.5.cloned.1.call-done = bf16[384,4096]{1,0:T(8,128)(2,1)} async-done(((bf16[48,4096]{1,0:T(8,128)(2,1)}), bf16[384,4096]{1,0:T(8,128)(2,1)}) %all-gather.5.cloned.1.call-update) | async-done | bytes 3145744 | tf_op jit(solution)/shard_map/all_gather | solution.py:83
  44.4 2.6 multiply_reduce_fusion.6
  47.0 29.6 %all-gather.3.cloned.1.call-done = bf16[384,4096]{1,0:T(8,128)(2,1)} async-done(((bf16[48,4096]{1,0:T(8,128)(2,1)}), bf16[384,4096]{1,0:T(8,128)(2,1)}) %all-gather.3.cloned.1.call-update) | async-done | bytes 3145744 | tf_op jit(solution)/shard_map/all_gather | solution.py:82
  76.7 2.6 multiply_reduce_fusion.7
  79.3 8.5 %fusion.8 = (f32[768]{0:T(1024)S(1)}, f32[768,4096]{1,0:T(8,128)}) fusion(f32[4096]{0:T(1024)S(1)} %add_sqrt_fusion, bf16[768,384]{1,0:T(8,128)(2,1)S(1)} %copy-done, bf16[384,4096]{1,0:T(8,128)(2,1)} %all-gather.5.cloned.1.call-done), kind=kOutput, calls=%fused_computation.43 | convolution fusion | flops 2422209792 | bytes 16337920 | tf_op jit(solution)/shard_map/dot_general | solution.py:91
  87.8 6.4 %fusion.3 = (f32[768]{0:T(1024)S(1)}, f32[768,4096]{1,0:T(8,128)}) fusion(f32[4096]{0:T(1024)S(1)} %add_sqrt_fusion.1, bf16[768,384]{1,0:T(8,128)(2,1)S(1)} %copy-done.3, bf16[384,4096]{1,0:T(8,128)(2,1)S(1)} %copy-done.1), kind=kOutput, calls=%fused_computation.18 | convolution fusion | flops 2422209792 | bytes 16337920 | tf_op jit(solution)/shard_map/dot_general | solution.py:88
  94.2 0.6 select_maximum_fusion.2.x_ref
  94.8 15.7 %shard_map.67 = f32[16,128]{1,0:T(8,128)} custom-call(f32[16,128]{1,0:T(8,128)} %select_maximum_fusion.2.x_ref), custom_call_target="tpu_custom_call" | custom-call | tf_op jit(solution)/shard_map/pallas_call | solution.py:55
  110.5 0.7 slice_bitcast_fusion
  111.2 16.0 %fusion.7 = (f32[4096]{0:T(1024)}, f32[768,4096]{1,0:T(8,128)}, f32[768]{0:T(1024)S(1)}) fusion(f32[768]{0:T(1024)S(1)} %get-tuple-element.16, f32[768,4096]{1,0:T(8,128)} %get-tuple-element.20, f32[4096]{0:T(1024)S(1)} %add_sqrt_fusion.1, f32[768,4096]{1,0:T(8,128)} %get-tuple-element.18, f32[768]{0:T(1024)S(1)} %get-tuple-element.15), kind=kLoop, calls=%fused_computation.42 | loop fusion | flops 22015232 | bytes 37790720 | tf_op jit(solution)/shard_map/reduce_sum | solution.py:105
  127.1 8.3 %shard_map.68 = f32[32,128]{1,0:T(8,128)} custom-call(f32[32,128]{1,0:T(8,128)} %bitcast.37), custom_call_target="tpu_custom_call" | custom-call | tf_op jit(solution)/shard_map/pallas_call | solution.py:55
  135.5 0.7 divide_bitcast_fusion.2
  136.2 5.6 %multiply_reduce_fusion.4 = f32[768]{0:T(1024)S(1)} fusion(f32[768,4096]{1,0:T(8,128)} %get-tuple-element.10, f32[4096]{0:T(1024)S(1)} %divide_bitcast_fusion.2), kind=kLoop, calls=%fused_computation.8 | loop fusion | flops 6290688 | bytes 12602368 | tf_op jit(solution)/shard_map/reduce_sum | solution.py:108
  141.8 0.6 fusion.4.x_ref
  142.4 14.0 %shard_map.69 = f32[16,128]{1,0:T(8,128)} custom-call(f32[16,128]{1,0:T(8,128)} %fusion.4.x_ref), custom_call_target="tpu_custom_call" | custom-call | tf_op jit(solution)/shard_map/pallas_call | solution.py:55
  156.3 0.7 divide_bitcast_fusion.5
  157.0 6.8 %multiply_reduce_fusion.3 = f32[4096]{0:T(1024)} fusion(f32[768,4096]{1,0:T(8,128)} %get-tuple-element.10, f32[768]{0:T(1024)S(1)} %divide_bitcast_fusion.5), kind=kLoop, calls=%fused_computation.5 | loop fusion | flops 6287360 | bytes 12602368 | tf_op jit(solution)/shard_map/reduce_sum | solution.py:105
  163.8 7.9 %shard_map.70 = f32[32,128]{1,0:T(8,128)} custom-call(f32[32,128]{1,0:T(8,128)} %bitcast.39), custom_call_target="tpu_custom_call" | custom-call | tf_op jit(solution)/shard_map/pallas_call | solution.py:55
  171.7 0.7 divide_bitcast_fusion.1
  172.4 5.6 %multiply_reduce_fusion.2 = f32[768]{0:T(1024)S(1)} fusion(f32[768,4096]{1,0:T(8,128)} %get-tuple-element.10, f32[4096]{0:T(1024)S(1)} %divide_bitcast_fusion.1), kind=kLoop, calls=%fused_computation.4 | loop fusion | flops 6290688 | bytes 12602368 | tf_op jit(solution)/shard_map/reduce_sum | solution.py:108
  178.0 0.6 select_maximum_fusion.1.x_ref
  178.6 15.0 %shard_map.71 = f32[16,128]{1,0:T(8,128)} custom-call(f32[16,128]{1,0:T(8,128)} %select_maximum_fusion.1.x_ref), custom_call_target="tpu_custom_call" | custom-call | tf_op jit(solution)/shard_map/pallas_call | solution.py:55
  193.6 0.7 divide_bitcast_fusion.4
  194.3 6.8 %multiply_reduce_fusion.1 = f32[4096]{0:T(1024)} fusion(f32[768,4096]{1,0:T(8,128)} %get-tuple-element.10, f32[768]{0:T(1024)S(1)} %divide_bitcast_fusion.4), kind=kLoop, calls=%fused_computation.3 | loop fusion | flops 6287360 | bytes 12602368 | tf_op jit(solution)/shard_map/reduce_sum | solution.py:105
  201.1 8.6 %shard_map.72 = f32[32,128]{1,0:T(8,128)} custom-call(f32[32,128]{1,0:T(8,128)} %bitcast.40), custom_call_target="tpu_custom_call" | custom-call | tf_op jit(solution)/shard_map/pallas_call | solution.py:55
  209.7 0.7 divide_bitcast_fusion
  210.4 5.5 %multiply_reduce_fusion.5 = f32[768]{0:T(1024)S(1)} fusion(f32[768,4096]{1,0:T(8,128)} %get-tuple-element.10, f32[4096]{0:T(1024)S(1)} %divide_bitcast_fusion), kind=kLoop, calls=%fused_computation.10 | loop fusion | flops 6290688 | bytes 12602368 | tf_op jit(solution)/shard_map/reduce_sum | solution.py:108
  215.9 0.6 select_maximum_fusion.x_ref
  216.5 13.4 %shard_map.73 = f32[16,128]{1,0:T(8,128)} custom-call(f32[16,128]{1,0:T(8,128)} %select_maximum_fusion.x_ref), custom_call_target="tpu_custom_call" | custom-call | tf_op jit(solution)/shard_map/pallas_call | solution.py:55
  229.9 0.7 log_bitcast_fusion
  230.6 13.1 %fusion.2 = f32[384,4096]{0,1:T(8,128)} fusion(bf16[768,384]{1,0:T(8,128)(2,1)S(1)} %copy-done, f32[768,4096]{1,0:T(8,128)} %get-tuple-element.18, f32[768,4096]{1,0:T(8,128)} %get-tuple-element.10, f32[768]{0:T(1024)S(1)} %get-tuple-element.13, f32[768]{0:T(1024)S(1)} %get-tuple-element.14, f32[4096]{0:T(1024)S(1)} %divide_bitcast_fusion, ...), kind=kOutput, calls=%fused_computation.17 | convolution fusion | flops 2444230656 | bytes 32072704 | tf_op jit(solution)/shard_map/dot_general | solution.py:121
  243.7 6.5 %copy.11 = f32[384,4096]{1,0:T(8,128)} copy(f32[384,4096]{0,1:T(8,128)} %fusion.2) | data formatting | bytes 12582912
  250.2 0.0 reduce-scatter.4.cloned.1.call-update
  250.2 14.4 %multiply_reduce_fusion = (f32[]{:T(128)}, bf16[768,4096]{1,0:T(8,128)(2,1)}) fusion(f32[768,4096]{1,0:T(8,128)} %get-tuple-element.18, f32[768,4096]{1,0:T(8,128)} %get-tuple-element.10, f32[768]{0:T(1024)S(1)} %get-tuple-element.13, f32[768]{0:T(1024)S(1)} %get-tuple-element.14, f32[4096]{0:T(1024)S(1)} %divide_bitcast_fusion, f32[768]{0:T(1024)S(1)} %get-tuple-element.15), kind=kLoop, calls=%fused_computation.1 | loop fusion | flops 28311552 | bytes 31482884 | tf_op jit(solution)/shard_map/reduce_sum | solution.py:116
  265.3 1.3 copy.9
  266.6 77.2 %psum.7 = f32[]{:T(128)} all-reduce(f32[]{:T(128)S(6)} %neg.3), channel_id=1, replica_groups=mesh['dp'=8,'proto'=32] {'dp','proto'}, use_global_device_ids=true, to_apply=%region_12.13 | all-reduce | flops 1 | bytes 8 | tf_op jit(solution)/shard_map/psum | solution.py:118
  344.5 0.0 reduce-scatter.4.cloned.1.call-done
  344.5 1.7 copy.12
  346.2 2.9 multiply_reduce_fusion.8
  349.2 7.4 %shard_map.74 = f32[32,128]{1,0:T(8,128)} custom-call(f32[32,128]{1,0:T(8,128)} %bitcast.41), custom_call_target="tpu_custom_call" | custom-call | tf_op jit(solution)/shard_map/pallas_call | solution.py:55
  356.5 5.2 %subtract_divide_fusion = f32[48,4096]{0,1:T(8,128)} fusion(f32[48,4096]{0,1:T(8,128)S(1)} %copy.12, bf16[48,4096]{0,1:T(8,128)(2,1)} %copy.9, f32[4096]{0:T(1024)} %bitcast.38, f32[4096]{0:T(1024)S(1)} %add_sqrt_fusion), kind=kLoop, calls=%fused_computation.19 | loop fusion | flops 983040 | bytes 1998848 | tf_op jit(solution)/shard_map/div | solution.py:129
  361.8 3.1 copy.10
  (9 shorter events, 0.0 us)
Async XLA Ops:
  7.2 72.1 %copy-start = (bf16[768,384]{1,0:T(8,128)(2,1)S(1)}, bf16[768,384]{1,0:T(8,128)(2,1)}, u32[]{:S(2)}) copy-start(bf16[768,384]{1,0:T(8,128)(2,1)} %param.5) | copy-start | bytes 1769476
  7.2 37.3 %all-gather.5.cloned.1.call-start = ((), (), s32[]{:S(2)}) async-start(), calls=%async_computation.2 | async-start | bytes 3538944 | tf_op jit(solution)/shard_map/all_gather | solution.py:83
  7.9 68.8 %all-gather.3.cloned.1.call-start = ((), (), s32[]{:S(2)}) async-start(), calls=%async_computation.1 | async-start | bytes 3538944 | tf_op jit(solution)/shard_map/all_gather | solution.py:82
  8.7 335.8 %reduce-scatter.4.cloned.1.call-start = ((), (), s32[]{:S(2)}) async-start(), calls=%async_computation.3 | async-start | bytes 7077888
  79.3 8.6 %copy-start.1 = (bf16[384,4096]{1,0:T(8,128)(2,1)S(1)}, bf16[384,4096]{1,0:T(8,128)(2,1)}, u32[]{:S(2)}) copy-start(bf16[384,4096]{1,0:T(8,128)(2,1)} %all-gather.3.cloned.1.call-done) | copy-start | bytes 9437188
  79.3 8.6 %copy-start.3 = (bf16[768,384]{1,0:T(8,128)(2,1)S(1)}, bf16[768,384]{1,0:T(8,128)(2,1)}, u32[]{:S(2)}) copy-start(bf16[768,384]{1,0:T(8,128)(2,1)} %param.4) | copy-start | bytes 1769476
  250.2 15.1 %copy-start.2 = (bf16[48,4096]{1,0:T(8,128)(2,1)S(1)}, bf16[48,4096]{1,0:T(8,128)(2,1)}, u32[]{:S(2)}) copy-start(bf16[48,4096]{1,0:T(8,128)(2,1)} %param.7) | copy-start | bytes 1179652
Sparse Core Ops, SparseCore 0:
  9.8 34.5 all-gather.4
  46.3 30.3 all-gather.2
  250.3 44.0 reduce-scatter.3

commit v2 on v0

v2 whole, which is shorter than its diff:
```python
import math

import jax
import jax.numpy as jnp
from jax import lax
from jax.experimental import pallas as pl
from jax.experimental.pallas import tpu as pltpu
from jax.sharding import PartitionSpec as P

ITERS = 3
teacher_temp = 0.07
student_temp = 0.1
norm_eps = 1e-06
MESH = pl.DeviceIdType.MESH
LOG2E = math.log2(math.e)
LN2 = math.log(2.0)
F32 = jnp.float32
BF16 = jnp.bfloat16

NY, NX, NZ = 4, 4, 8
NDP = 2 * NY
CROPS = 768
PROTOS = 4096
BOTTLE = 384
SLAB = BOTTLE // NDP
LANES = 128
GROUPS = PROTOS // LANES
CBLK = CROPS // LANES
NCHUNK = 4
CHUNK = PROTOS // NCHUNK
FCHUNK = 512
NF = PROTOS // FCHUNK
TOTAL_CROPS = CROPS * NDP
TOTAL_PROTOS = PROTOS * NX * NZ


def remote(src, dst, send, recv, **device):
    return pltpu.make_async_remote_copy(
        src_ref=src, dst_ref=dst, send_sem=send, recv_sem=recv, device_id=device, device_id_type=MESH
    )


def head_kernel(
    tf, sf, tw, sw,
    codes, loss_out, grad,
    TW, SW, Z, S, sfT, part, zcol, ccol, lcol, crow, prow, pstmp, isn,
    stage, sig, ownf, sendsib, recvsib, sendy, recvy,
    dbuf, dbuf4, xbuf, zbuf, xbuf3, zbuf3,
    local_sem, code_sem, t_send, t_recv, s_send, s_recv,
    d_send, d_recv, x_send, x_recv, z_send, z_recv, sib_send, sib_recv, y_send, y_recv,
):
    j = lax.axis_index("dp")
    p = lax.axis_index("proto")
    y, core = lax.div(j, 2), lax.rem(j, 2)
    z, x = lax.div(p, NX), lax.rem(p, NX)
    sib = 2 * y + (1 - core)

    def ypeer(o):
        return 2 * lax.rem(y + o, NY) + core

    def xpeer(o):
        return z * NX + lax.rem(x + o, NX)

    def zpeer(o):
        return lax.rem(z + o, NZ) * NX + x

    barrier = pltpu.get_barrier_semaphore()

    @pl.loop(1, NDP)
    def _(o):
        pl.semaphore_signal(barrier, inc=1, device_id={"dp": lax.rem(j + o, NDP)}, device_id_type=MESH)

    @pl.loop(1, NX)
    def _(o):
        pl.semaphore_signal(barrier, inc=1, device_id={"proto": xpeer(o)}, device_id_type=MESH)

    @pl.loop(1, NZ)
    def _(o):
        pl.semaphore_signal(barrier, inc=1, device_id={"proto": zpeer(o)}, device_id_type=MESH)

    pl.semaphore_wait(barrier, (NDP - 1) + (NX - 1) + (NZ - 1))

    def rows_of(index):
        return pl.ds(pl.multiple_of(index * SLAB, 16), SLAB)

    def cols_of(q):
        return pl.ds(pl.multiple_of(q * CHUNK, CHUNK), CHUNK)

    @pl.loop(0, NCHUNK)
    def _(q):
        src = tw.at[:, cols_of(q)]
        dst = TW.at[rows_of(j), cols_of(q)]
        remote(src, dst, t_send, t_recv.at[q, 0], dp=ypeer(1)).start()
        remote(src, dst, t_send, t_recv.at[q, 1], dp=ypeer(3)).start()
        remote(src, dst, t_send, t_recv.at[q, 4], dp=sib).start()

    own_t = pltpu.make_async_copy(tw, TW.at[rows_of(j)], local_sem.at[0])
    own_s = pltpu.make_async_copy(sw, SW.at[rows_of(j)], local_sem.at[1])
    own_t.start()
    own_s.start()

    for half in range(2):
        for slab in range(NY):
            index = 2 * slab + half
            block = sf[:, index * SLAB:(index + 1) * SLAB].astype(F32)
            sfT[half, slab * SLAB:(slab + 1) * SLAB, :] = jnp.transpose(block).astype(BF16)

    def t_wait(q, kind, index, half=None):
        if half is None:
            region = TW.at[rows_of(index), cols_of(q)]
        else:
            start = pl.multiple_of(q * CHUNK + half * (CHUNK // 2), CHUNK // 2)
            region = TW.at[rows_of(index), pl.ds(start, CHUNK // 2)]
        remote(region, region, t_send, t_recv.at[q, kind], dp=sib).wait_recv()
        return region

    left, right, far = ypeer(3), ypeer(1), ypeer(2)

    @pl.loop(0, NCHUNK)
    def _(q):
        region = t_wait(q, 0, left)
        a = TW.at[rows_of(left), pl.ds(pl.multiple_of(q * CHUNK, CHUNK), CHUNK // 2)]
        remote(a, a, t_send, t_recv.at[q, 2], dp=right).start()
        remote(region, region, t_send, t_recv.at[q, 5], dp=sib).start()
        region = t_wait(q, 1, right)
        b = TW.at[rows_of(right), pl.ds(pl.multiple_of(q * CHUNK + CHUNK // 2, CHUNK // 2), CHUNK // 2)]
        remote(b, b, t_send, t_recv.at[q, 3], dp=left).start()
        remote(region, region, t_send, t_recv.at[q, 6], dp=sib).start()

    mine = SW.at[rows_of(j)]
    for o in (1, 3, 2):
        remote(sw, mine, s_send, s_recv.at[o - 1], dp=ypeer(o)).start()
    remote(sw, mine, s_send, s_recv.at[3], dp=sib).start()
    own_t.wait()
    own_s.wait()

    def logits_chunk(q, feat, W, OUT, constant, keep):
        cols = cols_of(q)

        def square(r, acc):
            w = W[pl.ds(pl.multiple_of(r * 16, 16), 16), cols].astype(F32)
            w = w * w
            return acc + (w[:8] + w[8:])

        acc = lax.fori_loop(0, BOTTLE // 16, square, jnp.zeros((8, CHUNK), F32), unroll=4)
        inverse = 1.0 / jnp.sqrt(jnp.sum(acc, axis=0, keepdims=True) + norm_eps)
        if keep is not None:
            keep[:, cols] = jnp.broadcast_to(inverse, (8, CHUNK))
        crow[...] = jnp.broadcast_to(inverse * constant, (8, CHUNK))

        @pl.loop(0, CHUNK // 256)
        def _(b):
            inner = pl.ds(pl.multiple_of(q * CHUNK + b * 256, 256), 256)
            value = jnp.dot(feat[...], W[:, inner], preferred_element_type=F32)
            value = value * crow[0:1, pl.ds(pl.multiple_of(b * 256, 256), 256)]
            OUT[:, inner] = value
            part[...] = jnp.maximum(part[...], jnp.maximum(value[:, :128], value[:, 128:]))

    part[...] = jnp.full((CROPS, LANES), -jnp.inf, F32)

    @pl.loop(0, NCHUNK)
    def _(q):
        t_wait(q, 2, far, 0)
        t_wait(q, 3, far, 1)
        region = TW.at[rows_of(far), cols_of(q)]
        remote(region, region, t_send, t_recv.at[q, 7], dp=sib).start()

    @pl.loop(0, NCHUNK)
    def _(q):
        t_wait(q, 4, sib)
        for kind, o in ((5, 3), (6, 1), (7, 2)):
            t_wait(q, kind, 2 * lax.rem(y + o, NY) + (1 - core))
        logits_chunk(q, tf, TW, Z, LOG2E / teacher_temp, None)

    def start(axis, buf, me, n, peer, send, recv):
        @pl.loop(1, n)
        def _(o):
            slot = buf.at[me]
            remote(slot, slot, send, recv, **{axis: peer(o)}).start()

    def finish(axis, buf, n, peer, send, recv):
        region = buf.at[pl.ds(0, n - 1)]
        remote(region, region, send, recv, **{axis: peer(1)}).wait_recv()

    def done_sending(axis, buf, n, peer, send, recv):
        region = buf.at[pl.ds(0, n - 1)]
        remote(region, region, send, recv, **{axis: peer(1)}).wait_send()

    def dpeer(o):
        return lax.rem(j + o, NDP)

    sent = []

    def over_dp(i, buf):
        args = ("dp", buf, NDP, dpeer, d_send.at[i], d_recv.at[i])
        sent.append(args)
        start("dp", buf, j, NDP, dpeer, d_send.at[i], d_recv.at[i])
        return lambda: finish(*args)

    def over_x(i, buf):
        args = ("proto", buf, NX, xpeer, x_send.at[i], x_recv.at[i])
        sent.append(args)
        start("proto", buf, x, NX, xpeer, x_send.at[i], x_recv.at[i])
        return lambda: finish(*args)

    def over_z(i, buf):
        args = ("proto", buf, NZ, zpeer, z_send.at[i], z_recv.at[i])
        sent.append(args)
        start("proto", buf, z, NZ, zpeer, z_send.at[i], z_recv.at[i])
        return lambda: finish(*args)

    def combine(buf, n, op):
        total = buf[0]
        for k in range(1, n):
            total = op(total, buf[k])
        return total

    def lane_reduce(reduce):
        rows = []
        for i in range(CBLK):
            rows.append(reduce(jnp.transpose(part[i * LANES:(i + 1) * LANES, :]), axis=0, keepdims=True))
        rows.append(jnp.zeros((8 - CBLK, LANES), F32))
        return jnp.concatenate(rows, axis=0)

    def to_columns(value, out):
        for i in range(CBLK):
            out[i * LANES:(i + 1) * LANES, :] = jnp.transpose(jnp.broadcast_to(value[i:i + 1, :], (LANES, LANES)))

    def exp_rows(first, last):
        @pl.loop(first // 8, last // 8)
        def _(r):
            rows = pl.ds(pl.multiple_of(r * 8, 8), 8)
            peak = zcol[rows, :]
            for g in range(GROUPS):
                lanes = pl.ds(g * LANES, LANES)
                Z[rows, lanes] = jnp.exp2(Z[rows, lanes] - peak)

    def proto_pass(out):
        for seg in range(NCHUNK):
            n = CHUNK // LANES

            def step(r, acc):
                rows = pl.ds(pl.multiple_of(r * 8, 8), 8)
                c = ccol[rows, :]
                return tuple(
                    acc[g] + Z[rows, pl.ds(seg * CHUNK + g * LANES, LANES)] * c for g in range(n)
                )

            acc = lax.fori_loop(0, CROPS // 8, step, tuple(jnp.zeros((8, LANES), F32) for _ in range(n)), unroll=8)
            for g in range(n):
                out[pl.ds(seg * n + g, 1), :] = jnp.sum(acc[g], axis=0, keepdims=True)

    def crop_pass():
        @pl.loop(0, CROPS // 32)
        def _(r):
            acc = [jnp.zeros((8, LANES), F32) for _ in range(4)]
            for g in range(GROUPS):
                scale = prow[:, g * LANES:(g + 1) * LANES]
                for k in range(4):
                    rows = pl.ds(pl.multiple_of(r * 32 + k * 8, 8), 8)
                    acc[k] = acc[k] + Z[rows, pl.ds(g * LANES, LANES)] * scale
            for k in range(4):
                part[pl.ds(pl.multiple_of(r * 32 + k * 8, 8), 8), :] = acc[k]

    def student_relay():
        for k, o in ((0, 3), (2, 1), (1, 2)):
            region = SW.at[rows_of(ypeer(o))]
            remote(region, region, s_send, s_recv.at[k], dp=sib).wait_recv()
            remote(region, region, s_send, s_recv.at[4 + k], dp=sib).start()

    def student_arrived():
        region = SW.at[rows_of(sib)]
        remote(region, region, s_send, s_recv.at[3], dp=sib).wait_recv()
        for k, o in ((0, 3), (2, 1), (1, 2)):
            region = SW.at[rows_of(2 * lax.rem(y + o, NY) + (1 - core))]
            remote(region, region, s_send, s_recv.at[4 + k], dp=sib).wait_recv()

    def student_chunk(q):
        logits_chunk(q, sf, SW, S, LOG2E / student_temp, isn)

    def student_sums():
        peak = lane_reduce(jnp.max)
        to_columns(peak, lcol)

        @pl.loop(0, CROPS // 8)
        def _(r):
            rows = pl.ds(pl.multiple_of(r * 8, 8), 8)
            top = lcol[rows, :]
            acc = [jnp.zeros((8, LANES), F32) for _ in range(4)]
            for g in range(GROUPS):
                acc[g % 4] = acc[g % 4] + jnp.exp2(S[rows, pl.ds(g * LANES, LANES)] - top)
            part[rows, :] = (acc[0] + acc[1]) + (acc[2] + acc[3])
        return peak, lane_reduce(jnp.sum)

    own_peak = lane_reduce(jnp.max)
    xbuf[0, x] = own_peak
    wait = over_x(0, xbuf.at[0])
    to_columns(own_peak, zcol)
    exp_rows(0, CROPS // 2)
    wait()
    zbuf[0, z] = combine(xbuf.at[0], NX, jnp.maximum)
    wait = over_z(0, zbuf.at[0])
    exp_rows(CROPS // 2, CROPS)
    wait()
    peak = combine(zbuf.at[0], NZ, jnp.maximum)
    adjust = jnp.exp2(own_peak - peak)
    to_columns(adjust, ccol)

    for it in range(ITERS):
        proto_pass(dbuf.at[it, j])
        wait = over_dp(it, dbuf.at[it])
        if it == 1:
            student_arrived()
            part[...] = jnp.full((CROPS, LANES), -jnp.inf, F32)
            student_chunk(0)
            student_chunk(1)
            student_chunk(2)
            student_chunk(3)
        if it == 2:
            s_peak, s_sum = student_sums()
            xbuf3[x, 8:16] = s_peak
            xbuf3[x, 16:24] = s_sum
        wait()
        pstmp[...] = 1.0 / (TOTAL_PROTOS * combine(dbuf.at[it], NDP, jnp.add))
        for g in range(GROUPS):
            prow[:, g * LANES:(g + 1) * LANES] = jnp.broadcast_to(pstmp[g:g + 1, :], (8, LANES))
        if it == 1:
            zcol[...] = part[...]
        crop_pass()
        crop_local = lane_reduce(jnp.sum) * adjust
        if it == 1:
            part[...] = zcol[...]
        if it < 2:
            xbuf[1 + it, x] = crop_local
            wait = over_x(1 + it, xbuf.at[1 + it])
            if it == 0:
                student_relay()
            wait()
            zbuf[1 + it, z] = combine(xbuf.at[1 + it], NX, jnp.add)
            wait = over_z(1 + it, zbuf.at[1 + it])
            wait()
            crop_mass = combine(zbuf.at[1 + it], NZ, jnp.add)
        else:
            def merge(a, b):
                top = jnp.maximum(a[8:16], b[8:16])
                total = a[16:24] * jnp.exp2(a[8:16] - top) + b[16:24] * jnp.exp2(b[8:16] - top)
                return jnp.concatenate([a[0:8] + b[0:8], top, total], axis=0)

            xbuf3[x, 0:8] = crop_local
            wait = over_x(3, xbuf3)
            wait()
            zbuf3[z] = combine(xbuf3, NX, merge)
            wait = over_z(3, zbuf3)
            wait()
            merged = combine(zbuf3, NZ, merge)
            crop_mass = merged[0:8]
            lse = merged[8:16] + jnp.log2(merged[16:24])
        crop_scale = 1.0 / (TOTAL_CROPS * crop_mass)
        if it < 2:
            to_columns(crop_scale * adjust, ccol)
        else:
            to_columns(crop_scale * adjust * TOTAL_CROPS, ccol)
            to_columns(lse, lcol)

    def fcols(f):
        return pl.ds(pl.multiple_of(f * FCHUNK, FCHUNK), FCHUNK)

    def code_copy(f, slot):
        return pltpu.make_async_copy(stage.at[slot], codes.at[:, fcols(f)], code_sem.at[slot])

    def sib_copy(f):
        return remote(sendsib.at[:, :, fcols(f)], recvsib.at[:, :, fcols(f)], sib_send, sib_recv.at[f], dp=sib)

    def forward(f):
        sib_copy(f).wait_recv()
        for o in range(1, NY):
            to = lax.rem(y + o, NY)
            total = ownf[to, :, fcols(f)] + recvsib[to, :, fcols(f)].astype(F32)
            sendy[o - 1, :, fcols(f)] = total.astype(BF16)
            remote(
                sendy.at[o - 1, :, fcols(f)], recvy.at[o - 1, :, fcols(f)],
                y_send, y_recv.at[o - 1], dp=ypeer(o),
            ).start()

    @pl.loop(0, NF, init_carry=jnp.zeros((16, FCHUNK), F32))
    def loss_acc(f, loss_acc):
        slot = lax.rem(f, 2)

        @pl.when(f >= 2)
        def _():
            code_copy(f - 2, slot).wait()

        scale = jnp.broadcast_to(prow[0:1, fcols(f)], (16, FCHUNK))
        n = FCHUNK // LANES

        def step(r, carry):
            loss, pressure = carry
            rows = pl.ds(pl.multiple_of(r * 16, 16), 16)
            c = jnp.concatenate([ccol[rows, :]] * n, axis=1)
            l = jnp.concatenate([lcol[rows, :]] * n, axis=1)
            assign = Z[rows, fcols(f)] * scale * c
            stage[slot, rows, :] = assign.astype(BF16)
            s = S[rows, fcols(f)]
            logp = s - l
            signal = ((jnp.exp2(logp) - assign) * (1.0 / student_temp)).astype(BF16)
            sig[rows, :] = signal
            return loss + assign * logp, pressure + signal.astype(F32) * s

        loss_acc, pressure = lax.fori_loop(
            0, CROPS // 16, step, (loss_acc, jnp.zeros((16, FCHUNK), F32)), unroll=2
        )
        code_copy(f, slot).start()
        pressure = jnp.sum(pressure, axis=0, keepdims=True) * (LN2 * student_temp)
        for g in range(n):
            dbuf4[j, pl.ds(f * n + g, 1), :] = pressure[:, g * LANES:(g + 1) * LANES]
        other = jnp.dot(sfT[1 - core], sig[...], preferred_element_type=F32)
        sendsib[:, :, fcols(f)] = other.astype(BF16).reshape(NY, SLAB, FCHUNK)
        sib_copy(f).start()
        own = jnp.dot(sfT[core], sig[...], preferred_element_type=F32)
        ownf[:, :, fcols(f)] = own.reshape(NY, SLAB, FCHUNK)

        @pl.when(f >= 1)
        def _():
            forward(f - 1)
        return loss_acc

    forward(NF - 1)

    folded = loss_acc[0:8] + loss_acc[8:16]
    folded = (folded[:, 0:128] + folded[:, 128:256]) + (folded[:, 256:384] + folded[:, 384:512])
    dbuf4[j, GROUPS:GROUPS + 8] = folded
    wait = over_dp(3, dbuf4)
    wait()
    total = combine(dbuf4, NDP, jnp.add)
    xbuf[3, x] = total[GROUPS:]
    wait = over_x(4, xbuf.at[3])
    pstmp[...] = total[:GROUPS]
    wait()
    zbuf[3, z] = combine(xbuf.at[3], NX, jnp.add)
    wait = over_z(4, zbuf.at[3])
    wait()
    loss = combine(zbuf.at[3], NZ, jnp.add)
    loss = jnp.sum(jnp.sum(loss, axis=1, keepdims=True), axis=0, keepdims=True)
    loss_out[...] = jnp.broadcast_to(loss * (-LN2 / TOTAL_CROPS), (8, LANES))

    for o in range(1, NY):
        remote(sendy.at[o - 1], recvy.at[o - 1], y_send, y_recv.at[o - 1], dp=ypeer(o)).wait_recv()

    for f in range(NF):
        cols = slice(f * FCHUNK, (f + 1) * FCHUNK)
        pressure = jnp.concatenate(
            [pstmp[f * 4 + g:f * 4 + g + 1, :] for g in range(FCHUNK // LANES)], axis=1
        )
        inverse = isn[0:1, cols]
        direct = ownf[y, :, cols] + recvsib[y, :, cols].astype(F32)
        for o in range(NY - 1):
            direct = direct + recvy[o, :, cols].astype(F32)
        weight = sw_rows(SW, j, cols).astype(F32)
        grad[:, cols] = (direct - weight * (inverse * pressure)) * inverse

    code_copy(NF - 2, 0).wait()
    code_copy(NF - 1, 1).wait()
    for args in sent:
        done_sending(*args)
    region = TW.at[pl.ds(0, 7 * SLAB)]
    remote(region, region, t_send, t_recv.at[0, 0], dp=sib).wait_send()
    region = SW.at[pl.ds(0, 7 * SLAB)]
    remote(region, region, s_send, s_recv.at[0], dp=sib).wait_send()
    remote(sendsib, recvsib, sib_send, sib_recv.at[0], dp=sib).wait_send()
    remote(sendy, recvy, y_send, y_recv.at[0], dp=ypeer(1)).wait_send()


def sw_rows(SW, j, cols):
    return SW[pl.ds(pl.multiple_of(j * SLAB, 16), SLAB), cols]


def body(teacher_features, student_features, teacher_weight, student_weight):
    vmem = pl.BlockSpec(memory_space=pltpu.VMEM)
    hbm = pl.BlockSpec(memory_space=pl.ANY)
    dma = pltpu.SemaphoreType.DMA
    codes, loss, grad = pl.pallas_call(
        head_kernel,
        out_shape=(
            jax.ShapeDtypeStruct((CROPS, PROTOS), BF16),
            jax.ShapeDtypeStruct((8, LANES), F32),
            jax.ShapeDtypeStruct((SLAB, PROTOS), F32),
        ),
        in_specs=[vmem, vmem, hbm, hbm],
        out_specs=(hbm, vmem, vmem),
        scratch_shapes=[
            pltpu.VMEM((BOTTLE, PROTOS), BF16),
            pltpu.VMEM((BOTTLE, PROTOS), BF16),
            pltpu.VMEM((CROPS, PROTOS), F32),
            pltpu.VMEM((CROPS, PROTOS), F32),
            pltpu.VMEM((2, BOTTLE // 2, CROPS), BF16),
            pltpu.VMEM((CROPS, LANES), F32),
            pltpu.VMEM((CROPS, LANES), F32),
            pltpu.VMEM((CROPS, LANES), F32),
            pltpu.VMEM((CROPS, LANES), F32),
            pltpu.VMEM((8, CHUNK), F32),
            pltpu.VMEM((8, PROTOS), F32),
            pltpu.VMEM((GROUPS, LANES), F32),
            pltpu.VMEM((8, PROTOS), F32),
            pltpu.VMEM((2, CROPS, FCHUNK), BF16),
            pltpu.VMEM((CROPS, FCHUNK), BF16),
            pltpu.VMEM((NY, SLAB, PROTOS), F32),
            pltpu.VMEM((NY, SLAB, PROTOS), BF16),
            pltpu.VMEM((NY, SLAB, PROTOS), BF16),
            pltpu.VMEM((NY - 1, SLAB, PROTOS), BF16),
            pltpu.VMEM((NY - 1, SLAB, PROTOS), BF16),
            pltpu.VMEM((ITERS, NDP, GROUPS, LANES), F32),
            pltpu.VMEM((NDP, GROUPS + 8, LANES), F32),
            pltpu.VMEM((4, NX, 8, LANES), F32),
            pltpu.VMEM((4, NZ, 8, LANES), F32),
            pltpu.VMEM((NX, 24, LANES), F32),
            pltpu.VMEM((NZ, 24, LANES), F32),
            dma((2,)), dma((2,)), dma, dma((NCHUNK, 8)), dma, dma((7,)),
            dma((4,)), dma((4,)), dma((5,)), dma((5,)), dma((5,)), dma((5,)),
            dma, dma((NF,)), dma, dma((NY - 1,)),
        ],
        compiler_params=pltpu.CompilerParams(
            collective_id=0, has_side_effects=True, vmem_limit_bytes=60 * 1024 * 1024
        ),
    )(teacher_features, student_features, teacher_weight, student_weight)
    return codes, loss[0, 0], grad


def solution(mesh):
    return jax.shard_map(
        body,
        mesh=mesh,
        in_specs=(P("dp", None), P("dp", None), P("dp", "proto"), P("dp", "proto")),
        out_specs=(P("dp", "proto"), P(), P("dp", "proto")),
        check_vma=False,
    )
```

time: 689 us -> 132 us (0.19)
  blocking collectives: 454 us -> 0 us
  Pallas kernels: 0 us -> 123 us
  matrix products: 91 us -> 0 us
  waiting for transfers between devices: 66.8 us -> 0 us
  other arithmetic: 37 us -> 0 us
  between operations: 16.6 us -> 0.64 us
  local copies, waits for them, and re-layouts: 17.1 us -> 8.43 us
    psum x8 -> x0, blocking collectives: 391 us -> none  [the longest x3 171 us: body(): crop_mass = lax.psum(crop_local, 'proto')]
    pallas_call x0 -> x1, Pallas kernels: none -> 123 us  [body(): pl.pallas_call(head_kernel, out_shape=(jax.ShapeDtypeStruct((CROPS, PROTO...]
    dot_general x9 -> x0, matrix products: 91 us -> none  [the longest x3 39.9 us: body(): crop_local = jnp.dot(powers, proto_scale, precision=lax.Precision.HIGHEST)]
    all_gather x2 -> x0, waiting for transfers between devices: 65.4 us -> none  [the longest x1 35.7 us: body(): lax.all_gather(student_weight, 'dp', axis=0, tiled=True)]
    pmax x1 -> x0, blocking collectives: 62.7 us -> none  [body(): lax.pmax((jnp.max(teacher_logits, axis=1), jnp.max(student_logits, axis=1...]
    reduce_sum x5 -> x0, other arithmetic: 32.3 us -> none  [the longest x1 14.4 us: body(): loss_local = -jnp.sum(assign * log_prob)]
    unnamed x14 -> x4, local copies, waits for them, and re-layouts: 17.1 us -> 7.24 us
  transfers between devices with their start and end apart: 3 -> 0, of which waited for: 2 -> 0; matrix products, arithmetic and copies ran while one was open for 3% -> 0% of each run, Pallas kernels for 0% -> 0%
where the time goes in v2:
time: 132 us
  Pallas kernels  123 us (93%)
  local copies, waits for them, and re-layouts  8.43 us (6%)
    pallas_call x1, Pallas kernels, body(): pl.pallas_call(head_kernel, out_shape=(jax.ShapeDtypeStruct((CROPS, PROTO...  123 us
    unnamed x4, local copies, waits for them, and re-layouts  7.24 us

profile of v2, /device:TPU:1, one launch (start us, length us, event | category | flops | bytes accessed | tf_op | source)
XLA Modules:
  0.0 131.7 jit_solution(11969251481912707366)
XLA Ops:
  0.6 122.6 %shard_map.67 = (bf16[768,4096]{1,0:T(8,128)(2,1)}, f32[8,128]{1,0:T(8,128)}, f32[48,4096]{1,0:T(8,128)}) custom-call(bf16[768,384]{1,0:T(8,128)(2,1)} %tf.1, bf16[768,384]{1,0:T(8,128)(2,1)} %sf.1, bf16[48,4096]{1,0:T(8,128)(2,1)} %tw.1, bf16[48,4096]{1,0:T(8,128)(2,1)} %sw.1), custom_call_target="tpu_custom_call" | custom-call | tf_op jit(solution)/shard_map/pallas_call | solution.py:481
  123.3 1.2 slice.3
  124.4 0.0 copy-start
  124.4 6.4 %copy.9 = bf16[768,4096]{1,0:T(8,128)(2,1)} copy(bf16[768,4096]{1,0:T(8,128)(2,1)} %get-tuple-element.12) | data formatting | bytes 12582912
  130.8 0.0 copy-done
  130.8 0.9 copy.10
Async XLA Ops:
  124.4 6.4 %copy-start = (f32[48,4096]{1,0:T(8,128)S(1)}, f32[48,4096]{1,0:T(8,128)}, u32[]{:S(2)}) copy-start(f32[48,4096]{1,0:T(8,128)} %get-tuple-element.14) | copy-start | bytes 2359300

commit v3 on v2

--- a/solution.py
+++ b/solution.py
@@ -19,6 +19,7 @@
 
 NY, NX, NZ = 4, 4, 8
 NDP = 2 * NY
+NPR = NX * NZ
 CROPS = 768
 PROTOS = 4096
 BOTTLE = 384
@@ -30,8 +31,9 @@
 CHUNK = PROTOS // NCHUNK
 FCHUNK = 512
 NF = PROTOS // FCHUNK
+NWRITE = 4
 TOTAL_CROPS = CROPS * NDP
-TOTAL_PROTOS = PROTOS * NX * NZ
+TOTAL_PROTOS = PROTOS * NPR
 
 
 def remote(src, dst, send, recv, **device):
@@ -43,11 +45,11 @@
 def head_kernel(
     tf, sf, tw, sw,
     codes, loss_out, grad,
-    TW, SW, Z, S, sfT, part, zcol, ccol, lcol, crow, prow, pstmp, isn,
-    stage, sig, ownf, sendsib, recvsib, sendy, recvy,
-    dbuf, dbuf4, xbuf, zbuf, xbuf3, zbuf3,
-    local_sem, code_sem, t_send, t_recv, s_send, s_recv,
-    d_send, d_recv, x_send, x_recv, z_send, z_recv, sib_send, sib_recv, y_send, y_recv,
+    TW, SW, Z, S, sfT, part, spart, zcol, ccol, lcol, crow, prow, pstmp, isn,
+    sig, ownf, sendsib, recvsib, sendy, recvy,
+    dbuf, dbuf4, pbuf0, pbuf1, pbuf2, pbuf3,
+    local_sem, t_send, t_recv, s_send, s_recv,
+    d_send, d_recv, p_send, p_recv, sib_send, sib_recv, y_send, y_recv,
 ):
     j = lax.axis_index("dp")
     p = lax.axis_index("proto")
@@ -58,27 +60,26 @@
     def ypeer(o):
         return 2 * lax.rem(y + o, NY) + core
 
-    def xpeer(o):
-        return z * NX + lax.rem(x + o, NX)
-
-    def zpeer(o):
-        return lax.rem(z + o, NZ) * NX + x
+    def swing(i, n):
+        return n // 2 + lax.div(i + 1, 2) * (1 - 2 * lax.rem(i, 2))
+
+    def dpeer(i):
+        return 2 * lax.rem(y + swing(lax.div(i, 2), NY), NY) + lax.rem(core + 1 + i, 2)
+
+    def ppeer(i):
+        return lax.rem(z + swing(lax.div(i, NX), NZ), NZ) * NX + lax.rem(x + 1 + i, NX)
 
     barrier = pltpu.get_barrier_semaphore()
 
-    @pl.loop(1, NDP)
-    def _(o):
-        pl.semaphore_signal(barrier, inc=1, device_id={"dp": lax.rem(j + o, NDP)}, device_id_type=MESH)
-
-    @pl.loop(1, NX)
-    def _(o):
-        pl.semaphore_signal(barrier, inc=1, device_id={"proto": xpeer(o)}, device_id_type=MESH)
-
-    @pl.loop(1, NZ)
-    def _(o):
-        pl.semaphore_signal(barrier, inc=1, device_id={"proto": zpeer(o)}, device_id_type=MESH)
-
-    pl.semaphore_wait(barrier, (NDP - 1) + (NX - 1) + (NZ - 1))
+    @pl.loop(0, NPR - 1)
+    def _(i):
+        pl.semaphore_signal(barrier, inc=1, device_id={"proto": ppeer(i)}, device_id_type=MESH)
+
+    @pl.loop(0, NDP - 1)
+    def _(i):
+        pl.semaphore_signal(barrier, inc=1, device_id={"dp": dpeer(i)}, device_id_type=MESH)
+
+    pl.semaphore_wait(barrier, (NDP - 1) + (NPR - 1))
 
     def rows_of(index):
         return pl.ds(pl.multiple_of(index * SLAB, 16), SLAB)
@@ -134,7 +135,7 @@
     own_t.wait()
     own_s.wait()
 
-    def logits_chunk(q, feat, W, OUT, constant, keep):
+    def logits_chunk(q, feat, W, OUT, top, constant, keep):
         cols = cols_of(q)
 
         def square(r, acc):
@@ -154,60 +155,51 @@
             value = jnp.dot(feat[...], W[:, inner], preferred_element_type=F32)
             value = value * crow[0:1, pl.ds(pl.multiple_of(b * 256, 256), 256)]
             OUT[:, inner] = value
-            part[...] = jnp.maximum(part[...], jnp.maximum(value[:, :128], value[:, 128:]))
+            top[...] = jnp.maximum(top[...], jnp.maximum(value[:, :128], value[:, 128:]))
 
     part[...] = jnp.full((CROPS, LANES), -jnp.inf, F32)
-
-    @pl.loop(0, NCHUNK)
-    def _(q):
+    spart[...] = jnp.full((CROPS, LANES), -jnp.inf, F32)
+
+    def t_far(q):
         t_wait(q, 2, far, 0)
         t_wait(q, 3, far, 1)
         region = TW.at[rows_of(far), cols_of(q)]
         remote(region, region, t_send, t_recv.at[q, 7], dp=sib).start()
 
-    @pl.loop(0, NCHUNK)
-    def _(q):
+    def t_logits(q):
         t_wait(q, 4, sib)
         for kind, o in ((5, 3), (6, 1), (7, 2)):
             t_wait(q, kind, 2 * lax.rem(y + o, NY) + (1 - core))
-        logits_chunk(q, tf, TW, Z, LOG2E / teacher_temp, None)
-
-    def start(axis, buf, me, n, peer, send, recv):
-        @pl.loop(1, n)
-        def _(o):
-            slot = buf.at[me]
-            remote(slot, slot, send, recv, **{axis: peer(o)}).start()
-
-    def finish(axis, buf, n, peer, send, recv):
+        logits_chunk(q, tf, TW, Z, part, LOG2E / teacher_temp, None)
+
+    t_far(0)
+
+    @pl.loop(1, NCHUNK)
+    def _(q):
+        t_far(q)
+        t_logits(q - 1)
+
+    t_logits(NCHUNK - 1)
+
+    sent = []
+
+    def exchange(axis, buf, me, n, peer, send, recv):
+        slot = buf.at[me]
+
+        @pl.loop(0, n - 1)
+        def _(i):
+            remote(slot, slot, send, recv, **{axis: peer(i)}).start()
+
         region = buf.at[pl.ds(0, n - 1)]
-        remote(region, region, send, recv, **{axis: peer(1)}).wait_recv()
-
-    def done_sending(axis, buf, n, peer, send, recv):
-        region = buf.at[pl.ds(0, n - 1)]
-        remote(region, region, send, recv, **{axis: peer(1)}).wait_send()
-
-    def dpeer(o):
-        return lax.rem(j + o, NDP)
-
-    sent = []
+        whole = remote(region, region, send, recv, **{axis: peer(0)})
+        sent.append(whole)
+        return whole.wait_recv
 
     def over_dp(i, buf):
-        args = ("dp", buf, NDP, dpeer, d_send.at[i], d_recv.at[i])
-        sent.append(args)
-        start("dp", buf, j, NDP, dpeer, d_send.at[i], d_recv.at[i])
-        return lambda: finish(*args)
-
-    def over_x(i, buf):
-        args = ("proto", buf, NX, xpeer, x_send.at[i], x_recv.at[i])
-        sent.append(args)
-        start("proto", buf, x, NX, xpeer, x_send.at[i], x_recv.at[i])
-        return lambda: finish(*args)
-
-    def over_z(i, buf):
-        args = ("proto", buf, NZ, zpeer, z_send.at[i], z_recv.at[i])
-        sent.append(args)
-        start("proto", buf, z, NZ, zpeer, z_send.at[i], z_recv.at[i])
-        return lambda: finish(*args)
+        return exchange("dp", buf, j, NDP, dpeer, d_send.at[i], d_recv.at[i])
+
+    def over_proto(i, buf):
+        return exchange("proto", buf, p, NPR, ppeer, p_send.at[i], p_recv.at[i])
 
     def combine(buf, n, op):
         total = buf[0]
@@ -215,7 +207,7 @@
             total = op(total, buf[k])
         return total
 
-    def lane_reduce(reduce):
+    def lane_reduce(part, reduce):
         rows = []
         for i in range(CBLK):
             rows.append(reduce(jnp.transpose(part[i * LANES:(i + 1) * LANES, :]), axis=0, keepdims=True))
@@ -262,6 +254,23 @@
             for k in range(4):
                 part[pl.ds(pl.multiple_of(r * 32 + k * 8, 8), 8), :] = acc[k]
 
+    def crop_loss_pass():
+        @pl.loop(0, CROPS // 16)
+        def _(r):
+            acc = [jnp.zeros((8, LANES), F32) for _ in range(2)]
+            acc2 = [jnp.zeros((8, LANES), F32) for _ in range(2)]
+            rows = [pl.ds(pl.multiple_of(r * 16 + k * 8, 8), 8) for k in range(2)]
+            lse = [lcol[rows[k], :] for k in range(2)]
+            for g in range(GROUPS):
+                scale = prow[:, g * LANES:(g + 1) * LANES]
+                for k in range(2):
+                    value = Z[rows[k], pl.ds(g * LANES, LANES)] * scale
+                    acc[k] = acc[k] + value
+                    acc2[k] = acc2[k] + value * (S[rows[k], pl.ds(g * LANES, LANES)] - lse[k])
+            for k in range(2):
+                part[rows[k], :] = acc[k]
+                spart[rows[k], :] = acc2[k]
+
     def student_relay():
         for k, o in ((0, 3), (2, 1), (1, 2)):
             region = SW.at[rows_of(ypeer(o))]
@@ -276,10 +285,10 @@
             remote(region, region, s_send, s_recv.at[4 + k], dp=sib).wait_recv()
 
     def student_chunk(q):
-        logits_chunk(q, sf, SW, S, LOG2E / student_temp, isn)
+        logits_chunk(q, sf, SW, S, spart, LOG2E / student_temp, isn)
 
     def student_sums():
-        peak = lane_reduce(jnp.max)
+        peak = lane_reduce(spart, jnp.max)
         to_columns(peak, lcol)
 
         @pl.loop(0, CROPS // 8)
@@ -289,84 +298,73 @@
             acc = [jnp.zeros((8, LANES), F32) for _ in range(4)]
             for g in range(GROUPS):
                 acc[g % 4] = acc[g % 4] + jnp.exp2(S[rows, pl.ds(g * LANES, LANES)] - top)
-            part[rows, :] = (acc[0] + acc[1]) + (acc[2] + acc[3])
-        return peak, lane_reduce(jnp.sum)
-
-    own_peak = lane_reduce(jnp.max)
-    xbuf[0, x] = own_peak
-    wait = over_x(0, xbuf.at[0])
+            spart[rows, :] = (acc[0] + acc[1]) + (acc[2] + acc[3])
+        return peak, lane_reduce(spart, jnp.sum)
+
+    own_peak = lane_reduce(part, jnp.max)
+    pbuf0[p] = own_peak
+    wait = over_proto(0, pbuf0)
     to_columns(own_peak, zcol)
-    exp_rows(0, CROPS // 2)
+    exp_rows(0, CROPS)
     wait()
-    zbuf[0, z] = combine(xbuf.at[0], NX, jnp.maximum)
-    wait = over_z(0, zbuf.at[0])
-    exp_rows(CROPS // 2, CROPS)
-    wait()
-    peak = combine(zbuf.at[0], NZ, jnp.maximum)
+    peak = combine(pbuf0, NPR, jnp.maximum)
     adjust = jnp.exp2(own_peak - peak)
     to_columns(adjust, ccol)
 
     for it in range(ITERS):
         proto_pass(dbuf.at[it, j])
         wait = over_dp(it, dbuf.at[it])
+        if it == 0:
+            student_relay()
         if it == 1:
-            student_arrived()
-            part[...] = jnp.full((CROPS, LANES), -jnp.inf, F32)
-            student_chunk(0)
-            student_chunk(1)
-            student_chunk(2)
-            student_chunk(3)
-        if it == 2:
+            student_chunk(NCHUNK - 1)
             s_peak, s_sum = student_sums()
-            xbuf3[x, 8:16] = s_peak
-            xbuf3[x, 16:24] = s_sum
+            pbuf2[p, 8:16] = s_peak
+            pbuf2[p, 16:24] = s_sum
         wait()
         pstmp[...] = 1.0 / (TOTAL_PROTOS * combine(dbuf.at[it], NDP, jnp.add))
         for g in range(GROUPS):
             prow[:, g * LANES:(g + 1) * LANES] = jnp.broadcast_to(pstmp[g:g + 1, :], (8, LANES))
-        if it == 1:
-            zcol[...] = part[...]
-        crop_pass()
-        crop_local = lane_reduce(jnp.sum) * adjust
-        if it == 1:
-            part[...] = zcol[...]
         if it < 2:
-            xbuf[1 + it, x] = crop_local
-            wait = over_x(1 + it, xbuf.at[1 + it])
-            if it == 0:
-                student_relay()
+            crop_pass()
+        else:
+            crop_loss_pass()
+        crop_local = lane_reduce(part, jnp.sum) * adjust
+        if it == 0:
+            pbuf1[p] = crop_local
+            wait = over_proto(1, pbuf1)
+            student_arrived()
+            for q in range(NCHUNK - 1):
+                student_chunk(q)
             wait()
-            zbuf[1 + it, z] = combine(xbuf.at[1 + it], NX, jnp.add)
-            wait = over_z(1 + it, zbuf.at[1 + it])
-            wait()
-            crop_mass = combine(zbuf.at[1 + it], NZ, jnp.add)
+            crop_mass = combine(pbuf1, NPR, jnp.add)
+        elif it == 1:
+            pbuf2[p, 0:8] = crop_local
+            over_proto(2, pbuf2)()
+            crop_mass, top = pbuf2[0, 0:8], pbuf2[0, 8:16]
+            for k in range(1, NPR):
+                crop_mass = crop_mass + pbuf2[k, 0:8]
+                top = jnp.maximum(top, pbuf2[k, 8:16])
+            total = jnp.zeros((8, LANES), F32)
+            for k in range(NPR):
+                total = total + pbuf2[k, 16:24] * jnp.exp2(pbuf2[k, 8:16] - top)
+            to_columns(top + jnp.log2(total), lcol)
         else:
-            def merge(a, b):
-                top = jnp.maximum(a[8:16], b[8:16])
-                total = a[16:24] * jnp.exp2(a[8:16] - top) + b[16:24] * jnp.exp2(b[8:16] - top)
-                return jnp.concatenate([a[0:8] + b[0:8], top, total], axis=0)
-
-            xbuf3[x, 0:8] = crop_local
-            wait = over_x(3, xbuf3)
-            wait()
-            zbuf3[z] = combine(xbuf3, NX, merge)
-            wait = over_z(3, zbuf3)
-            wait()
-            merged = combine(zbuf3, NZ, merge)
-            crop_mass = merged[0:8]
-            lse = merged[8:16] + jnp.log2(merged[16:24])
+            pbuf3[p, 0:8] = crop_local
+            pbuf3[p, 8:16] = lane_reduce(spart, jnp.sum) * adjust
+            over_proto(3, pbuf3)()
+            both = combine(pbuf3, NPR, jnp.add)
+            crop_mass = both[0:8]
         crop_scale = 1.0 / (TOTAL_CROPS * crop_mass)
         if it < 2:
             to_columns(crop_scale * adjust, ccol)
         else:
             to_columns(crop_scale * adjust * TOTAL_CROPS, ccol)
-            to_columns(lse, lcol)
+            crop_loss = (crop_scale * both[8:16])[0:CBLK]
+            dbuf4[j, GROUPS:GROUPS + 8] = jnp.concatenate([crop_loss, jnp.zeros((8 - CBLK, LANES), F32)], axis=0)
 
     def fcols(f):
         return pl.ds(pl.multiple_of(f * FCHUNK, FCHUNK), FCHUNK)
-
-    def code_copy(f, slot):
-        return pltpu.make_async_copy(stage.at[slot], codes.at[:, fcols(f)], code_sem.at[slot])
 
     def sib_copy(f):
         return remote(sendsib.at[:, :, fcols(f)], recvsib.at[:, :, fcols(f)], sib_send, sib_recv.at[f], dp=sib)
@@ -382,34 +380,24 @@
                 y_send, y_recv.at[o - 1], dp=ypeer(o),
             ).start()
 
-    @pl.loop(0, NF, init_carry=jnp.zeros((16, FCHUNK), F32))
-    def loss_acc(f, loss_acc):
-        slot = lax.rem(f, 2)
-
-        @pl.when(f >= 2)
-        def _():
-            code_copy(f - 2, slot).wait()
-
+    @pl.loop(0, NF)
+    def _(f):
         scale = jnp.broadcast_to(prow[0:1, fcols(f)], (16, FCHUNK))
         n = FCHUNK // LANES
 
-        def step(r, carry):
-            loss, pressure = carry
+        def step(r, pressure):
             rows = pl.ds(pl.multiple_of(r * 16, 16), 16)
             c = jnp.concatenate([ccol[rows, :]] * n, axis=1)
             l = jnp.concatenate([lcol[rows, :]] * n, axis=1)
             assign = Z[rows, fcols(f)] * scale * c
-            stage[slot, rows, :] = assign.astype(BF16)
+            codes[rows, fcols(f)] = assign.astype(BF16)
             s = S[rows, fcols(f)]
             logp = s - l
             signal = ((jnp.exp2(logp) - assign) * (1.0 / student_temp)).astype(BF16)
             sig[rows, :] = signal
-            return loss + assign * logp, pressure + signal.astype(F32) * s
-
-        loss_acc, pressure = lax.fori_loop(
-            0, CROPS // 16, step, (loss_acc, jnp.zeros((16, FCHUNK), F32)), unroll=2
-        )
-        code_copy(f, slot).start()
+            return pressure + signal.astype(F32) * s
+
+        pressure = lax.fori_loop(0, CROPS // 16, step, jnp.zeros((16, FCHUNK), F32), unroll=2)
         pressure = jnp.sum(pressure, axis=0, keepdims=True) * (LN2 * student_temp)
         for g in range(n):
             dbuf4[j, pl.ds(f * n + g, 1), :] = pressure[:, g * LANES:(g + 1) * LANES]
@@ -422,26 +410,13 @@
         @pl.when(f >= 1)
         def _():
             forward(f - 1)
-        return loss_acc
-
+
+    wait = over_dp(3, dbuf4)
     forward(NF - 1)
-
-    folded = loss_acc[0:8] + loss_acc[8:16]
-    folded = (folded[:, 0:128] + folded[:, 128:256]) + (folded[:, 256:384] + folded[:, 384:512])
-    dbuf4[j, GROUPS:GROUPS + 8] = folded
-    wait = over_dp(3, dbuf4)
     wait()
     total = combine(dbuf4, NDP, jnp.add)
-    xbuf[3, x] = total[GROUPS:]
-    wait = over_x(4, xbuf.at[3])
     pstmp[...] = total[:GROUPS]
-    wait()
-    zbuf[3, z] = combine(xbuf.at[3], NX, jnp.add)
-    wait = over_z(4, zbuf.at[3])
-    wait()
-    loss = combine(zbuf.at[3], NZ, jnp.add)
-    loss = jnp.sum(jnp.sum(loss, axis=1, keepdims=True), axis=0, keepdims=True)
-    loss_out[...] = jnp.broadcast_to(loss * (-LN2 / TOTAL_CROPS), (8, LANES))
+    loss_out[0, 0] = jnp.sum(total[GROUPS:]) * (-LN2)
 
     for o in range(1, NY):
         remote(sendy.at[o - 1], recvy.at[o - 1], y_send, y_recv.at[o - 1], dp=ypeer(o)).wait_recv()
@@ -458,16 +433,26 @@
         weight = sw_rows(SW, j, cols).astype(F32)
         grad[:, cols] = (direct - weight * (inverse * pressure)) * inverse
 
-    code_copy(NF - 2, 0).wait()
-    code_copy(NF - 1, 1).wait()
-    for args in sent:
-        done_sending(*args)
+    for whole in sent:
+        whole.wait_send()
     region = TW.at[pl.ds(0, 7 * SLAB)]
     remote(region, region, t_send, t_recv.at[0, 0], dp=sib).wait_send()
     region = SW.at[pl.ds(0, 7 * SLAB)]
     remote(region, region, s_send, s_recv.at[0], dp=sib).wait_send()
     remote(sendsib, recvsib, sib_send, sib_recv.at[0], dp=sib).wait_send()
     remote(sendy, recvy, y_send, y_recv.at[0], dp=ypeer(1)).wait_send()
+
+
+def write_kernel(codes, grad, codes_out, grad_out, code_sem, grad_sem):
+    rows = CROPS // NWRITE
+    copies = [pltpu.make_async_copy(grad, grad_out, grad_sem)]
+    for i in range(NWRITE):
+        part = pl.ds(i * rows, rows)
+        copies.append(pltpu.make_async_copy(codes.at[part], codes_out.at[part], code_sem.at[i]))
+    for copy in copies:
+        copy.start()
+    for copy in copies:
+        copy.wait()
 
 
 def sw_rows(SW, j, cols):
@@ -481,12 +466,12 @@
     codes, loss, grad = pl.pallas_call(
         head_kernel,
         out_shape=(
-            jax.ShapeDtypeStruct((CROPS, PROTOS), BF16),
-            jax.ShapeDtypeStruct((8, LANES), F32),
-            jax.ShapeDtypeStruct((SLAB, PROTOS), F32),
+            pltpu.VMEM((CROPS, PROTOS), BF16),
+            jax.ShapeDtypeStruct((1, 1), F32),
+            pltpu.VMEM((SLAB, PROTOS), F32),
         ),
         in_specs=[vmem, vmem, hbm, hbm],
-        out_specs=(hbm, vmem, vmem),
+        out_specs=(vmem, pl.BlockSpec(memory_space=pltpu.SMEM), vmem),
         scratch_shapes=[
             pltpu.VMEM((BOTTLE, PROTOS), BF16),
             pltpu.VMEM((BOTTLE, PROTOS), BF16),
@@ -497,11 +482,11 @@
             pltpu.VMEM((CROPS, LANES), F32),
             pltpu.VMEM((CROPS, LANES), F32),
             pltpu.VMEM((CROPS, LANES), F32),
+            pltpu.VMEM((CROPS, LANES), F32),
             pltpu.VMEM((8, CHUNK), F32),
             pltpu.VMEM((8, PROTOS), F32),
             pltpu.VMEM((GROUPS, LANES), F32),
             pltpu.VMEM((8, PROTOS), F32),
-            pltpu.VMEM((2, CROPS, FCHUNK), BF16),
             pltpu.VMEM((CROPS, FCHUNK), BF16),
             pltpu.VMEM((NY, SLAB, PROTOS), F32),
             pltpu.VMEM((NY, SLAB, PROTOS), BF16),
@@ -510,18 +495,29 @@
             pltpu.VMEM((NY - 1, SLAB, PROTOS), BF16),
             pltpu.VMEM((ITERS, NDP, GROUPS, LANES), F32),
             pltpu.VMEM((NDP, GROUPS + 8, LANES), F32),
-            pltpu.VMEM((4, NX, 8, LANES), F32),
-            pltpu.VMEM((4, NZ, 8, LANES), F32),
-            pltpu.VMEM((NX, 24, LANES), F32),
-            pltpu.VMEM((NZ, 24, LANES), F32),
-            dma((2,)), dma((2,)), dma, dma((NCHUNK, 8)), dma, dma((7,)),
-            dma((4,)), dma((4,)), dma((5,)), dma((5,)), dma((5,)), dma((5,)),
+            pltpu.VMEM((NPR, 8, LANES), F32),
+            pltpu.VMEM((NPR, 8, LANES), F32),
+            pltpu.VMEM((NPR, 24, LANES), F32),
+            pltpu.VMEM((NPR, 16, LANES), F32),
+            dma((2,)), dma, dma((NCHUNK, 8)), dma, dma((7,)),
+            dma((4,)), dma((4,)), dma((4,)), dma((4,)),
             dma, dma((NF,)), dma, dma((NY - 1,)),
         ],
         compiler_params=pltpu.CompilerParams(
-            collective_id=0, has_side_effects=True, vmem_limit_bytes=60 * 1024 * 1024
+            collective_id=0, has_side_effects=True, vmem_limit_bytes=52 * 1024 * 1024
         ),
     )(teacher_features, student_features, teacher_weight, student_weight)
+    codes, grad = pl.pallas_call(
+        write_kernel,
+        out_shape=(
+            jax.ShapeDtypeStruct((CROPS, PROTOS), BF16),
+            jax.ShapeDtypeStruct((SLAB, PROTOS), F32),
+        ),
+        in_specs=[vmem, vmem],
+        out_specs=(hbm, hbm),
+        scratch_shapes=[dma((NWRITE,)), dma],
+        compiler_params=pltpu.CompilerParams(vmem_limit_bytes=1024 * 1024),
+    )(codes, grad)
     return codes, loss[0, 0], grad
 
 

time: 132 us -> 122 us (0.924)
  local copies, waits for them, and re-layouts: 8.43 us -> 0 us
  Pallas kernels: 123 us -> 120 us
  between operations: 0.64 us -> 2.4 us
    unnamed x4 -> x0, local copies, waits for them, and re-layouts: 7.24 us -> none
    pallas_call x1 -> x2, Pallas kernels: 123 us -> 120 us  [the longest x1 117 us: body(): pl.pallas_call(head_kernel, out_shape=(pltpu.VMEM((CROPS, PROTOS), BF16),...]
where the time goes in v3:
time: 122 us
  Pallas kernels  120 us (98%)
  between operations  2.4 us (2%)
    pallas_call x1, Pallas kernels, body(): pl.pallas_call(head_kernel, out_shape=(pltpu.VMEM((CROPS, PROTOS), BF16),...  117 us
    pallas_call x1, Pallas kernels, body(): pl.pallas_call(write_kernel, out_shape=(jax.ShapeDtypeStruct((CROPS, PROT...  2.98 us

profile of v3, /device:TPU:1, one launch (start us, length us, event | category | flops | bytes accessed | tf_op | source)
XLA Modules:
  0.0 122.0 jit_solution(813534403243021447)
XLA Ops:
  0.6 116.6 %shard_map.67 = (bf16[768,4096]{1,0:T(8,128)(2,1)S(1)}, f32[1,1]{1,0:T(1,128)}, f32[48,4096]{1,0:T(8,128)S(1)}) custom-call(bf16[768,384]{1,0:T(8,128)(2,1)} %tf.1, bf16[768,384]{1,0:T(8,128)(2,1)} %sf.1, bf16[48,4096]{1,0:T(8,128)(2,1)} %tw.1, bf16[48,4096]{1,0:T(8,128)(2,1)} %sw.1), custom_call_target="tpu_custom_call" | custom-call | tf_op jit(solution)/shard_map/pallas_call | solution.py:466
  117.2 3.0 %shard_map.68 = (bf16[768,4096]{1,0:T(8,128)(2,1)}, f32[48,4096]{1,0:T(8,128)}) custom-call(bf16[768,4096]{1,0:T(8,128)(2,1)S(1)} %get-tuple-element.8.codes, f32[48,4096]{1,0:T(8,128)S(1)} %get-tuple-element.9.grad), custom_call_target="tpu_custom_call" | custom-call | tf_op jit(solution)/shard_map/pallas_call | solution.py:510

commit v4 on v3

--- a/solution.py
+++ b/solution.py
@@ -369,16 +369,38 @@
     def sib_copy(f):
         return remote(sendsib.at[:, :, fcols(f)], recvsib.at[:, :, fcols(f)], sib_send, sib_recv.at[f], dp=sib)
 
+    def via(f):
+        return jnp.where(lax.rem(f, 2) == 0, right, left), jnp.where(lax.rem(f, 2) == 0, left, right)
+
+    def y_copy(f, kind, to):
+        return remote(
+            sendy.at[kind, :, fcols(f)], recvy.at[kind, :, fcols(f)], y_send, y_recv.at[kind, f], dp=to
+        )
+
+    def chip_sum(index, f):
+        slab = lax.div(index, 2)
+        return ownf[slab, :, fcols(f)] + recvsib[slab, :, fcols(f)]
+
     def forward(f):
         sib_copy(f).wait_recv()
-        for o in range(1, NY):
-            to = lax.rem(y + o, NY)
-            total = ownf[to, :, fcols(f)] + recvsib[to, :, fcols(f)].astype(F32)
-            sendy[o - 1, :, fcols(f)] = total.astype(BF16)
-            remote(
-                sendy.at[o - 1, :, fcols(f)], recvy.at[o - 1, :, fcols(f)],
-                y_send, y_recv.at[o - 1], dp=ypeer(o),
-            ).start()
+        near, away = via(f)
+        sendy[0, :, fcols(f)] = chip_sum(far, f).astype(BF16)
+        y_copy(f, 0, near).start()
+        sendy[1, :, fcols(f)] = chip_sum(away, f).astype(BF16)
+        y_copy(f, 1, away).start()
+
+    def forward_direct(f):
+        sib_copy(f).wait_recv()
+        near, away = via(f)
+        for kind, to in ((0, far), (1, away), (2, near)):
+            sendy[kind, :, fcols(f)] = chip_sum(to, f).astype(BF16)
+            y_copy(f, kind, to).start()
+
+    def pass_on(f):
+        near, away = via(f)
+        y_copy(f, 0, near).wait_recv()
+        sendy[2, :, fcols(f)] = (chip_sum(near, f) + recvy[0, :, fcols(f)].astype(F32)).astype(BF16)
+        y_copy(f, 2, near).start()
 
     @pl.loop(0, NF)
     def _(f):
@@ -402,34 +424,42 @@
         for g in range(n):
             dbuf4[j, pl.ds(f * n + g, 1), :] = pressure[:, g * LANES:(g + 1) * LANES]
         other = jnp.dot(sfT[1 - core], sig[...], preferred_element_type=F32)
-        sendsib[:, :, fcols(f)] = other.astype(BF16).reshape(NY, SLAB, FCHUNK)
+        sendsib[:, :, fcols(f)] = other.reshape(NY, SLAB, FCHUNK)
         sib_copy(f).start()
         own = jnp.dot(sfT[core], sig[...], preferred_element_type=F32)
         ownf[:, :, fcols(f)] = own.reshape(NY, SLAB, FCHUNK)
 
-        @pl.when(f >= 1)
+        @pl.when(f >= 2)
         def _():
-            forward(f - 1)
+            forward(f - 2)
+
+        @pl.when(f >= 4)
+        def _():
+            pass_on(f - 4)
 
     wait = over_dp(3, dbuf4)
-    forward(NF - 1)
+    forward_direct(NF - 2)
+    pass_on(NF - 4)
+    forward_direct(NF - 1)
+    pass_on(NF - 3)
     wait()
     total = combine(dbuf4, NDP, jnp.add)
     pstmp[...] = total[:GROUPS]
     loss_out[0, 0] = jnp.sum(total[GROUPS:]) * (-LN2)
 
-    for o in range(1, NY):
-        remote(sendy.at[o - 1], recvy.at[o - 1], y_send, y_recv.at[o - 1], dp=ypeer(o)).wait_recv()
-
     for f in range(NF):
         cols = slice(f * FCHUNK, (f + 1) * FCHUNK)
+        y_copy(f, 1, left).wait_recv()
+        y_copy(f, 2, left).wait_recv()
         pressure = jnp.concatenate(
             [pstmp[f * 4 + g:f * 4 + g + 1, :] for g in range(FCHUNK // LANES)], axis=1
         )
         inverse = isn[0:1, cols]
-        direct = ownf[y, :, cols] + recvsib[y, :, cols].astype(F32)
-        for o in range(NY - 1):
-            direct = direct + recvy[o, :, cols].astype(F32)
+        direct = ownf[y, :, cols] + recvsib[y, :, cols]
+        direct = direct + (recvy[1, :, cols].astype(F32) + recvy[2, :, cols].astype(F32))
+        if f >= NF - 2:
+            y_copy(f, 0, left).wait_recv()
+            direct = direct + recvy[0, :, cols].astype(F32)
         weight = sw_rows(SW, j, cols).astype(F32)
         grad[:, cols] = (direct - weight * (inverse * pressure)) * inverse
 
@@ -440,7 +470,7 @@
     region = SW.at[pl.ds(0, 7 * SLAB)]
     remote(region, region, s_send, s_recv.at[0], dp=sib).wait_send()
     remote(sendsib, recvsib, sib_send, sib_recv.at[0], dp=sib).wait_send()
-    remote(sendy, recvy, y_send, y_recv.at[0], dp=ypeer(1)).wait_send()
+    remote(sendy, recvy, y_send, y_recv.at[0, 0], dp=right).wait_send()
 
 
 def write_kernel(codes, grad, codes_out, grad_out, code_sem, grad_sem):
@@ -489,8 +519,8 @@
             pltpu.VMEM((8, PROTOS), F32),
             pltpu.VMEM((CROPS, FCHUNK), BF16),
             pltpu.VMEM((NY, SLAB, PROTOS), F32),
-            pltpu.VMEM((NY, SLAB, PROTOS), BF16),
-            pltpu.VMEM((NY, SLAB, PROTOS), BF16),
+            pltpu.VMEM((NY, SLAB, PROTOS), F32),
+            pltpu.VMEM((NY, SLAB, PROTOS), F32),
             pltpu.VMEM((NY - 1, SLAB, PROTOS), BF16),
             pltpu.VMEM((NY - 1, SLAB, PROTOS), BF16),
             pltpu.VMEM((ITERS, NDP, GROUPS, LANES), F32),
@@ -501,10 +531,10 @@
             pltpu.VMEM((NPR, 16, LANES), F32),
             dma((2,)), dma, dma((NCHUNK, 8)), dma, dma((7,)),
             dma((4,)), dma((4,)), dma((4,)), dma((4,)),
-            dma, dma((NF,)), dma, dma((NY - 1,)),
+            dma, dma((NF,)), dma, dma((NY - 1, NF)),
         ],
         compiler_params=pltpu.CompilerParams(
-            collective_id=0, has_side_effects=True, vmem_limit_bytes=52 * 1024 * 1024
+            collective_id=0, has_side_effects=True, vmem_limit_bytes=54 * 1024 * 1024
         ),
     )(teacher_features, student_features, teacher_weight, student_weight)
     codes, grad = pl.pallas_call(

time: 122 us -> 120 us (0.984)
  Pallas kernels: 120 us -> 117 us
    pallas_call x1, Pallas kernels: 117 us -> 114 us  [body(): pl.pallas_call(head_kernel, out_shape=(pltpu.VMEM((CROPS, PROTOS), BF16),...]
where the time goes in v4:
time: 120 us; the launch traced here: 119 us
  Pallas kernels  117 us (98%)
  between operations  2.4 us (2%)
    pallas_call x1, Pallas kernels, body(): pl.pallas_call(head_kernel, out_shape=(pltpu.VMEM((CROPS, PROTOS), BF16),...  114 us
    pallas_call x1, Pallas kernels, body(): pl.pallas_call(write_kernel, out_shape=(jax.ShapeDtypeStruct((CROPS, PROT...  2.98 us

profile of v4, /device:TPU:1, one launch (start us, length us, event | category | flops | bytes accessed | tf_op | source)
XLA Modules:
  0.0 119.5 jit_solution(13067942328083595459)
XLA Ops:
  0.6 114.1 %shard_map.67 = (bf16[768,4096]{1,0:T(8,128)(2,1)S(1)}, f32[1,1]{1,0:T(1,128)}, f32[48,4096]{1,0:T(8,128)S(1)}) custom-call(bf16[768,384]{1,0:T(8,128)(2,1)} %tf.1, bf16[768,384]{1,0:T(8,128)(2,1)} %sf.1, bf16[48,4096]{1,0:T(8,128)(2,1)} %tw.1, bf16[48,4096]{1,0:T(8,128)(2,1)} %sw.1), custom_call_target="tpu_custom_call" | custom-call | tf_op jit(solution)/shard_map/pallas_call | solution.py:496
  114.7 3.0 %shard_map.68 = (bf16[768,4096]{1,0:T(8,128)(2,1)}, f32[48,4096]{1,0:T(8,128)}) custom-call(bf16[768,4096]{1,0:T(8,128)(2,1)S(1)} %get-tuple-element.8.codes, f32[48,4096]{1,0:T(8,128)S(1)} %get-tuple-element.9.grad), custom_call_target="tpu_custom_call" | custom-call | tf_op jit(solution)/shard_map/pallas_call | solution.py:540

commit v5 on v4

--- a/solution.py
+++ b/solution.py
@@ -149,7 +149,7 @@
             keep[:, cols] = jnp.broadcast_to(inverse, (8, CHUNK))
         crow[...] = jnp.broadcast_to(inverse * constant, (8, CHUNK))
 
-        @pl.loop(0, CHUNK // 256)
+        @pl.loop(0, CHUNK // 256, unroll=2)
         def _(b):
             inner = pl.ds(pl.multiple_of(q * CHUNK + b * 256, 256), 256)
             value = jnp.dot(feat[...], W[:, inner], preferred_element_type=F32)
@@ -419,7 +419,7 @@
             sig[rows, :] = signal
             return pressure + signal.astype(F32) * s
 
-        pressure = lax.fori_loop(0, CROPS // 16, step, jnp.zeros((16, FCHUNK), F32), unroll=2)
+        pressure = lax.fori_loop(0, CROPS // 16, step, jnp.zeros((16, FCHUNK), F32), unroll=4)
         pressure = jnp.sum(pressure, axis=0, keepdims=True) * (LN2 * student_temp)
         for g in range(n):
             dbuf4[j, pl.ds(f * n + g, 1), :] = pressure[:, g * LANES:(g + 1) * LANES]

time: 120 us -> 119 us (level)
    pallas_call x1, Pallas kernels: 114 us -> 113 us  [body(): pl.pallas_call(head_kernel, out_shape=(pltpu.VMEM((CROPS, PROTOS), BF16),...]
where the time goes in v5:
time: 119 us; the launch traced here: 118 us
  Pallas kernels  116 us (97%)
  between operations  2.4 us (2%)
    pallas_call x1, Pallas kernels, body(): pl.pallas_call(head_kernel, out_shape=(pltpu.VMEM((CROPS, PROTOS), BF16),...  113 us
    pallas_call x1, Pallas kernels, body(): pl.pallas_call(write_kernel, out_shape=(jax.ShapeDtypeStruct((CROPS, PROT...  2.98 us

profile of v5, /device:TPU:1, one launch (start us, length us, event | category | flops | bytes accessed | tf_op | source)
XLA Modules:
  0.0 118.2 jit_solution(9838859737022969592)
XLA Ops:
  0.6 112.9 %shard_map.67 = (bf16[768,4096]{1,0:T(8,128)(2,1)S(1)}, f32[1,1]{1,0:T(1,128)}, f32[48,4096]{1,0:T(8,128)S(1)}) custom-call(bf16[768,384]{1,0:T(8,128)(2,1)} %tf.1, bf16[768,384]{1,0:T(8,128)(2,1)} %sf.1, bf16[48,4096]{1,0:T(8,128)(2,1)} %tw.1, bf16[48,4096]{1,0:T(8,128)(2,1)} %sw.1), custom_call_target="tpu_custom_call" | custom-call | tf_op jit(solution)/shard_map/pallas_call | solution.py:496
  113.5 3.0 %shard_map.68 = (bf16[768,4096]{1,0:T(8,128)(2,1)}, f32[48,4096]{1,0:T(8,128)}) custom-call(bf16[768,4096]{1,0:T(8,128)(2,1)S(1)} %get-tuple-element.8.codes, f32[48,4096]{1,0:T(8,128)S(1)} %get-tuple-element.9.grad), custom_call_target="tpu_custom_call" | custom-call | tf_op jit(solution)/shard_map/pallas_call | solution.py:540
